TPU v7x, 32 devices: a whole 2x2x4 slice. The times are simulated.
32 devices in a mesh: groups: 2 (over y), sec: 4 (over z), tile: 2 (over x), row: 2 (over core).
Axes of the slice: x: 2, y: 2, z: 4, core: 2. Of those that a mesh axis runs over, the one named last changes fastest.
Arguments:
- section_pixels: float32 [8, 512, 4096], P(('groups', 'sec'), ('tile', 'row')), parts along dimension 0, may hold values from -40 to 40
- jitter_index: int32 [8, 512], P(('groups', 'sec'), ('tile', 'row')), parts along dimension 0, may hold values from 0 to 7
- drift_list: int32 [8, 4, 8, 3], P(('groups', 'sec')), parts along dimension 0, may hold values from 0 to 31, as said below
- blend_weight: float32 [8, 4, 8], P(('groups', 'sec')), parts along dimension 0, may hold values from 0.5 to 2
- patch_col: int32 [4, 8], P(('tile', 'row'), 'groups'), parts along dimension 1, may hold values from 0 to 896
Outputs:
- jitter_phase: float32 [8, 512], P(('groups', 'sec'), ('tile', 'row')), parts along dimension 0
- surfaces: float32 [6, 4, 4, 128, 128], P('groups', ('tile', 'row'), 'sec'), parts along dimension 0
There are 2 independent parts, one for each index of `groups`. A program takes and returns all parts, laid end to end along the dimension named above; each array names one. Nothing has to cross between parts.
Inputs may be any that keep to these rules, and one draw needn't show every extreme that they name: `drift_list`: entry [s, j, k] names a block of band j (distinct over k), the band that owns its target, and the target block. No band sends more than 2 blocks to one owner, and in every section one owner receives exactly 2 blocks from every band.
All inputs are finite; a program needn't handle non-finite values.
Results may differ from a plain program's by a relative error of at most 0.0065.
Values may be sent and summed in bfloat16 or wider, within the bound.
A program may use at most 64 MiB of HBM per device.

v0:
```python
import functools
import math

import jax
import jax.numpy as jnp
import numpy as np
from jax import lax
from jax.experimental import pallas as pl
from jax.experimental.pallas import tpu as pltpu
from jax.sharding import PartitionSpec as P

SEG = 512
PATCH = 128
BLOCK = 128
CAP = 2
LANES = 128
MESH = pl.DeviceIdType.MESH


def dft_tables(side):
    index = np.arange(side)
    angles = (index[:, None] * index[None, :] % side) * (2.0 * math.pi / side)
    cosine, sine = np.cos(angles), np.sin(angles)
    table = np.concatenate(
        [
            np.concatenate([cosine, sine], 1),
            np.concatenate([cosine, -sine], 1),
            np.concatenate([-sine, -cosine], 1),
        ],
        0,
    )
    high = table.astype(jnp.bfloat16)
    low = (table - high.astype(np.float64)).astype(jnp.bfloat16)
    return np.stack([high, low])


def dot(a, b):
    return jnp.dot(a, b, preferred_element_type=jnp.float32)


def split(a):
    high = a.astype(jnp.bfloat16)
    return high, (a - high.astype(jnp.float32)).astype(jnp.bfloat16)


def dot3(a, b):
    return dot(a[0], b[0]) + (dot(a[0], b[1]) + dot(a[1], b[0]))


def kernel(
    sizes,
    pixels,
    delays_hbm,
    drifts_hbm,
    weights_hbm,
    columns_hbm,
    tables_hbm,
    jitter_out,
    freq,
    tables,
    raw,
    delays,
    drifts,
    weights,
    columns,
    delay_rows,
    aligned,
    slopes,
    cross_sums,
    energies,
    jitter_rows,
    halo_out,
    halo_in,
    outbox,
    arrived,
    patch_out,
    patch_in,
    load_sem,
    table_sem,
    small_sem,
    halo_send,
    halo_recv,
    block_send,
    block_recv,
    patch_send,
    patch_recv,
):
    sections, tiles, rows_axis, row_count, row_width, moves, chunks = sizes
    owners = tiles * rows_axis
    blocks = row_width // LANES
    groups = row_count // 8
    chunk_rows = row_count // chunks
    per_seg = SEG // LANES
    tile, row_at = lax.axis_index("tile"), lax.axis_index("row")
    me = tile * rows_axis + row_at
    section = lax.axis_index("sec")

    def band_device(band):
        return {"tile": band // rows_axis, "row": band % rows_axis}

    band_steps = [(t, r) for t in range(tiles) for r in range(rows_axis)][1:]
    band_steps.sort(key=lambda step: -min(step[0], tiles - step[0]))

    def band_at(step):
        return (tile + step[0]) % tiles * rows_axis + (row_at + step[1]) % rows_axis

    def band_from(step):
        return (tile - step[0] + tiles) % tiles * rows_axis + (
            row_at - step[1] + rows_axis
        ) % rows_axis

    section_steps = sorted(range(1, sections), key=lambda step: -min(step, sections - step))

    table_copy = pltpu.make_async_copy(tables_hbm, tables, table_sem)
    loads = [
        pltpu.make_async_copy(
            pixels.at[0, pl.ds(c * chunk_rows, chunk_rows)],
            raw.at[pl.ds(c * chunk_rows, chunk_rows)],
            load_sem.at[c],
        )
        for c in range(chunks)
    ]
    small_copies = [
        pltpu.make_async_copy(source, target, small_sem.at[i])
        for i, (source, target) in enumerate(
            (
                (delays_hbm, delays),
                (drifts_hbm, drifts),
                (weights_hbm, weights),
                (columns_hbm, columns),
            )
        )
    ]
    small_copies[0].start()
    loads[chunks - 1].start()
    for c in range(chunks - 1):
        loads[c].start()
    for copy in small_copies[1:]:
        copy.start()
    table_copy.start()

    barrier = pltpu.get_barrier_semaphore()
    for step in range(1, owners):
        pl.semaphore_signal(
            barrier, inc=1, device_id=band_device((me + step) % owners), device_id_type=MESH
        )
    for step in range(1, sections):
        pl.semaphore_signal(
            barrier, inc=1, device_id={"sec": (section + step) % sections}, device_id_type=MESH
        )

    lane = lax.broadcasted_iota(jnp.int32, (8, LANES), 1)
    first_lane, last_lane = lane == 0, lane == LANES - 1
    small_copies[0].wait()
    delay_rows[...] = jnp.broadcast_to(
        delays[...].astype(jnp.float32), (LANES, row_count)
    ).T
    zero = jnp.zeros((8, LANES), jnp.float32)
    for block in range(blocks):
        aligned[block, 0:8, :] = zero

    def align(start):
        delay = delay_rows[pl.ds(start, 8), :].astype(jnp.int32)
        values = [raw[pl.ds(start, 8), v * LANES : (v + 1) * LANES] for v in range(blocks)]
        index = lane + delay
        kept = index < LANES
        index = index & (LANES - 1)
        turned = [jnp.take_along_axis(x, index, axis=1) for x in values] + [zero]
        values = [jnp.where(kept, turned[v], turned[v + 1]) for v in range(blocks)]
        return values

    def differences(values):
        before = [pltpu.roll(x, 1, 1) for x in values]
        after = [pltpu.roll(x, LANES - 1, 1) for x in values]
        line, ring = [], []
        for v in range(blocks):
            left = jnp.where(first_lane, before[v - 1] if v else zero, before[v])
            right = jnp.where(last_lane, after[v + 1] if v < blocks - 1 else zero, after[v])
            line.append(right - left)
            if v % per_seg == 0:
                left = jnp.where(first_lane, before[v + per_seg - 1], before[v])
            if v % per_seg == per_seg - 1:
                right = jnp.where(last_lane, after[v - per_seg + 1], after[v])
            ring.append(right - left)
        return line, ring

    def total(terms):
        terms = list(terms)
        while len(terms) > 1:
            terms = [
                terms[i] + terms[i + 1] if i + 1 < len(terms) else terms[i]
                for i in range(0, len(terms), 2)
            ]
        return terms[0]

    loads[chunks - 1].wait()
    last = align(row_count - 8)
    for v in range(blocks):
        halo_out[v, :, :] = last[v]
    pl.semaphore_wait(barrier, owners + sections - 2)
    halo = pltpu.make_async_remote_copy(
        src_ref=halo_out.at[:, pl.ds(7, 1)],
        dst_ref=halo_in,
        send_sem=halo_send,
        recv_sem=halo_recv,
        device_id=band_device((me + 1) % owners),
        device_id_type=MESH,
    )
    halo.start()

    def group_step(g, carry):
        start = pl.multiple_of(g * 8, 8)
        values = align(start)
        for v in range(blocks):
            aligned[v, pl.ds(start + 8, 8), :] = values[v]
        line, ring = differences(values)
        for v in range(blocks):
            slopes[v, pl.ds(start, 8), :] = 0.5 * line[v]
        energies[pl.ds(start + 8, 8), :] = total(x * x for x in values)
        cross_sums[pl.ds(start, 8), :] = total(
            aligned[v, pl.ds(start + 7, 8), :] * ring[v] for v in range(blocks)
        )
        return carry

    def find(band, owner, rank):
        source, target, weight = jnp.int32(0), jnp.int32(-1), jnp.float32(0.0)
        seen = jnp.int32(0)
        for k in range(moves):
            hit = drifts[0, 1, band, k] == owner
            here = hit & (seen == rank)
            source = jnp.where(here, drifts[0, 0, band, k], source)
            target = jnp.where(here, drifts[0, 2, band, k], target)
            weight = jnp.where(here, weights[0, band, k], weight)
            seen = seen + hit.astype(jnp.int32)
        return source, target, weight

    for copy in small_copies[1:]:
        copy.wait()
    sources = {}
    for step in band_steps + [(0, 0)]:
        for rank in range(CAP):
            sources[step, rank] = find(me, band_at(step), rank)[0]

    segs = row_width // SEG

    def corrected(block, rows):
        shifted = slice(rows.start + 8, rows.stop + 8)
        return (
            aligned[block, shifted, :] - jitter_rows[rows, :] * slopes[block, rows, :]
        ).astype(jnp.bfloat16)

    block_copies = {}

    def finish_chunk(c):
        rows = slice(c * chunk_rows, (c + 1) * chunk_rows)
        numerator = jnp.sum(cross_sums[rows, :], axis=1, keepdims=True) * (-0.5 / segs)
        power = energies[rows.start + 8 : rows.stop + 8, :]
        power = power + energies[rows.start + 7 : rows.stop + 7, :]
        power = jnp.sum(power, axis=1, keepdims=True) * (0.5 / segs)
        jitter_rows[rows, :] = jnp.broadcast_to(numerator / (power + 1e-05), (chunk_rows, LANES))
        for step in band_steps:
            slot = step[0] * rows_axis + step[1]
            for rank in range(CAP):
                outbox[slot, rank, rows, :] = corrected(sources[step, rank], rows)
            copy = pltpu.make_async_remote_copy(
                src_ref=outbox.at[slot, :, pl.ds(rows.start, chunk_rows)],
                dst_ref=arrived.at[slot, :, pl.ds(rows.start, chunk_rows)],
                send_sem=block_send.at[slot, c],
                recv_sem=block_recv.at[slot, c],
                device_id=band_device(band_at(step)),
                device_id_type=MESH,
            )
            copy.start()
            block_copies[step, c] = copy

    def finish_first():
        _, ring0 = differences([aligned[v, 8:16, :] for v in range(blocks)])
        halo.wait_recv()
        is_first = me == 0
        above = [
            jnp.where(is_first, 0.0, jnp.broadcast_to(halo_in[v], (8, LANES))) for v in range(blocks)
        ]
        row = lax.broadcasted_iota(jnp.int32, (8, LANES), 0)
        cross_sums[0:8, :] = jnp.where(
            row == 0, total(above[v] * ring0[v] for v in range(blocks)), cross_sums[0:8, :]
        )
        energies[0:8, :] = total(a * a for a in above)
        finish_chunk(0)
    per_chunk = groups // chunks
    for c in range(chunks):
        if c < chunks - 1:
            loads[c].wait()
        lax.fori_loop(c * per_chunk, (c + 1) * per_chunk, group_step, 0)
        if c:
            finish_chunk(c)
        if c == chunks - 2:
            finish_first()

    chunk_order = list(range(1, chunks - 1)) + [0, chunks - 1]

    slab_blocks = blocks // sections
    slabs = [(section + step) % sections for step in range(sections)]
    offsets = [columns[0, slab] for slab in slabs]
    under = []
    for step in range(sections):
        block = slabs[step] * slab_blocks + offsets[step] // LANES
        under += [block, jnp.minimum(block + 1, blocks - 1)]
    norms = [jnp.float32(1.0)] * len(under)
    shares = {}
    for step in [(0, 0)] + band_steps:
        for rank in range(CAP):
            _, target, weight = find(band_from(step), me, rank)
            shares[step, rank] = [jnp.where(target == block, weight, 0.0) for block in under]
            norms = [norm + share for norm, share in zip(norms, shares[step, rank])]
    lanes = lax.broadcasted_iota(jnp.int32, (chunk_rows, LANES), 1)
    patch_copies = {}
    scales = [1.0 / jnp.full((1, LANES), norm) for norm in norms]
    for c in chunk_order:
        rows = slice(c * chunk_rows, (c + 1) * chunk_rows)
        terms = {}
        for rank in range(CAP):
            terms[(0, 0), rank] = corrected(sources[(0, 0), rank], rows).astype(jnp.float32)
        for step in band_steps[::-1]:
            block_copies[step, c].wait_recv()
            slot = step[0] * rows_axis + step[1]
            for rank in range(CAP):
                terms[step, rank] = arrived[slot, rank, rows, :].astype(jnp.float32)

        def merged(i):
            value = corrected(under[i], rows).astype(jnp.float32)
            for key, term in terms.items():
                value = value + shares[key][i] * term
            return value * scales[i]

        for step in section_steps + [0]:
            index = lanes + offsets[step] % LANES
            turn = index & (LANES - 1)
            patch = jnp.where(
                index < LANES,
                jnp.take_along_axis(merged(2 * step), turn, axis=1),
                jnp.take_along_axis(merged(2 * step + 1), turn, axis=1),
            ).astype(jnp.bfloat16)
            if step:
                patch_out[step, rows, :] = patch
                copy = pltpu.make_async_remote_copy(
                    src_ref=patch_out.at[step, pl.ds(rows.start, chunk_rows)],
                    dst_ref=patch_in.at[step, pl.ds(rows.start, chunk_rows)],
                    send_sem=patch_send.at[step, c],
                    recv_sem=patch_recv.at[step, c],
                    device_id={"sec": slabs[step]},
                    device_id_type=MESH,
                )
                copy.start()
                patch_copies[step, c] = copy
            else:
                patch_in[0, rows, :] = patch
    jitter_out[...] = jitter_rows[...].T[0:1, :]

    table_copy.wait()
    wide = tables[0, 0:PATCH, :], tables[1, 0:PATCH, :]
    square = tables[0, PATCH : 3 * PATCH, :], tables[1, PATCH : 3 * PATCH, :]
    def transform(steps):
        patches = jnp.concatenate([patch_in[step] for step in steps], 0)
        first = dot(patches, wide[0]) + dot(patches, wide[1])
        stacked = [
            jnp.concatenate([first[at : at + PATCH, :PATCH], first[at : at + PATCH, PATCH:]], 0)
            for at in range(0, len(steps) * PATCH, PATCH)
        ]
        both = dot3(square, split(jnp.concatenate(stacked, 1)))
        for i, step in enumerate(steps):
            source = (section - step + sections) % sections
            freq[source] = both[:, i * PATCH : (i + 1) * PATCH]

    transform([0])
    for step in section_steps[::-1]:
        for c in chunk_order:
            patch_copies[step, c].wait_recv()
    transform(section_steps[::-1])

    halo.wait_send()
    for copy in list(block_copies.values()) + list(patch_copies.values()):
        copy.wait_send()


def correlate(freq, tables, jitter, jitter_out, surfaces_out):
    jitter_out[...] = jitter[...]
    wide = tables[0, 0:PATCH, :]
    square = tables[0, PATCH : 3 * PATCH, :]
    for s in range(freq.shape[0] - 1):
        now_real, now_imag = freq[s, 0:PATCH], freq[s, PATCH : 2 * PATCH]
        next_real, next_imag = freq[s + 1, 0:PATCH], freq[s + 1, PATCH : 2 * PATCH]
        cross_real = now_real * next_real + now_imag * next_imag
        cross_imag = now_imag * next_real - now_real * next_imag
        magnitude = jnp.sqrt(cross_real * cross_real + cross_imag * cross_imag)
        mean = jnp.sum(jnp.sum(magnitude, axis=0, keepdims=True), axis=1, keepdims=True) * (
            1.0 / (PATCH * PATCH)
        )
        scaled = 1.0 / (magnitude + (0.5 * mean + 1e-06))
        damped = jnp.concatenate([cross_real * scaled, cross_imag * scaled], 1)
        back = dot(damped.astype(jnp.bfloat16), square)
        stacked = jnp.concatenate([back[:, :PATCH], back[:, PATCH:]], 0)
        surfaces_out[s, 0, 0] = dot(wide, stacked.astype(jnp.bfloat16)) * (1.0 / PATCH)


def per_device(section_pixels, jitter_index, drift_list, blend_weight, patch_col):
    _, row_count, row_width = section_pixels.shape
    sections = lax.axis_size("sec")
    tiles, rows_axis = lax.axis_size("tile"), lax.axis_size("row")
    owners = tiles * rows_axis
    moves = drift_list.shape[2]
    blocks = row_width // LANES
    chunks = 4
    sizes = (sections, tiles, rows_axis, row_count, row_width, moves, chunks)
    tables = dft_tables(PATCH)
    f32, bf16 = jnp.float32, jnp.bfloat16
    vmem = pl.BlockSpec(memory_space=pltpu.VMEM)
    anywhere = pl.BlockSpec(memory_space=pl.ANY)
    dma = pltpu.SemaphoreType.DMA
    between = pl.pallas_call(
        functools.partial(kernel, sizes),
        out_shape=(
            pltpu.VMEM((1, row_count), f32),
            pltpu.VMEM((sections, 2 * PATCH, PATCH), f32),
            pltpu.VMEM(tables.shape, bf16),
        ),
        in_specs=[anywhere] * 6,
        out_specs=(vmem, vmem, vmem),
        scratch_shapes=[
            pltpu.VMEM((row_count, row_width), f32),
            pltpu.VMEM(jitter_index.shape, jnp.int32),
            pltpu.SMEM((1, 3, owners, moves), jnp.int32),
            pltpu.SMEM(blend_weight.shape, f32),
            pltpu.SMEM(patch_col.shape, jnp.int32),
            pltpu.VMEM((row_count, LANES), f32),
            pltpu.VMEM((blocks, row_count + 8, LANES), f32),
            pltpu.VMEM((blocks, row_count, LANES), f32),
            pltpu.VMEM((row_count, LANES), f32),
            pltpu.VMEM((row_count + 8, LANES), f32),
            pltpu.VMEM((row_count, LANES), f32),
            pltpu.VMEM((blocks, 8, LANES), f32),
            pltpu.VMEM((blocks, 1, LANES), f32),
            pltpu.VMEM((owners, CAP, BLOCK, BLOCK), bf16),
            pltpu.VMEM((owners, CAP, BLOCK, BLOCK), bf16),
            pltpu.VMEM((sections, PATCH, PATCH), bf16),
            pltpu.VMEM((sections, PATCH, PATCH), bf16),
            dma((chunks,)),
            dma,
            dma((4,)),
            dma,
            dma,
            dma((owners, chunks)),
            dma((owners, chunks)),
            dma((sections, chunks)),
            dma((sections, chunks)),
        ],
        compiler_params=pltpu.CompilerParams(collective_id=0, has_side_effects=True),
        name="section_patches",
    )(
        section_pixels,
        jitter_index,
        jnp.transpose(drift_list, (0, 3, 1, 2)),
        blend_weight,
        patch_col,
        tables,
    )
    jitter, freq, tables = [pltpu.with_memory_space_constraint(x, pltpu.VMEM) for x in between]
    return pl.pallas_call(
        correlate,
        out_shape=(
            jax.ShapeDtypeStruct((1, row_count), f32),
            jax.ShapeDtypeStruct((sections - 1, 1, 1, PATCH, PATCH), f32),
        ),
        in_specs=[vmem] * 3,
        out_specs=(vmem, vmem),
        name="section_correlation",
    )(freq, tables, jitter)


def solution(mesh):
    in_specs = (
        P(("groups", "sec"), ("tile", "row"), None),
        P(("groups", "sec"), ("tile", "row")),
        P(("groups", "sec"), None, None, None),
        P(("groups", "sec"), None, None),
        P(("tile", "row"), "groups"),
    )
    out_specs = (
        P(("groups", "sec"), ("tile", "row")),
        P("groups", ("tile", "row"), "sec", None, None),
    )
    return jax.shard_map(
        per_device, mesh=mesh, in_specs=in_specs, out_specs=out_specs, check_vma=False
    )
```

profile of v0, /device:TPU:0, one launch (start us, length us, event | category | flops | bytes accessed | tf_op | source)
XLA Modules:
  0.0 19.0 jit_solution(4307998951002889450)
XLA Ops:
  0.6 17.0 %section_patches.1 = (f32[1,128]{1,0:T(1,128)S(1)}, f32[4,256,128]{2,1,0:T(8,128)S(1)}, bf16[2,384,256]{2,1,0:T(8,128)(2,1)S(1)}) custom-call(f32[1,128,4096]{2,1,0:T(8,128)} %pixels.1, s32[1,128]{1,0:T(1,128)} %delays_hbm.1, s32[1,3,4,8]{3,2,1,0:T(4,128)} %bitcast.1, f32[1,4,8]{2,1,0:T(4,128)} %weights_hbm.1, s32[1,4]{1,0:T(1,128)} %columns_hbm.1, ...), custom_call_target="tpu_custom_call" | custom-call | tf_op jit(solution)/shard_map/section_patches/pallas_call | solution.py:419
  17.6 1.3 %section_correlation.1 = (f32[1,128]{1,0:T(1,128)}, f32[3,1,1,128,128]{4,3,2,1,0:T(8,128)}) custom-call(f32[4,256,128]{2,1,0:T(8,128)S(1)} %get-tuple-element.5.freq, bf16[2,384,256]{2,1,0:T(8,128)(2,1)S(1)} %get-tuple-element.6.tables, f32[1,128]{1,0:T(1,128)S(1)} %get-tuple-element.7.jitter), custom_call_target="tpu_custom_call" | custom-call | tf_op jit(solution)/shard_map/section_correlation/pallas_call | solution.py:467
where the time goes:
time: 19.1 us; the launch traced here: 19 us
  Pallas kernels  18.3 us (96%)
  between operations  0.64 us (3%)
    pallas_call x1, Pallas kernels, per_device(): pl.pallas_call(functools.partial(kernel, sizes), out_shape=(pltpu.VMEM((1...  17 us
    pallas_call x1, Pallas kernels, per_device(): pl.pallas_call(correlate, out_shape=(jax.ShapeDtypeStruct((1, row_count),...  1.34 us

commit v1 on v0

v1 whole, which is shorter than its diff:
```python
import functools
import math

import jax
import jax.numpy as jnp
import numpy as np
from jax import lax
from jax.experimental import pallas as pl
from jax.experimental.pallas import tpu as pltpu
from jax.sharding import PartitionSpec as P

SEG = 512
PATCH = 128
BLOCK = 128
CAP = 2
LANES = 128
MESH = pl.DeviceIdType.MESH


def dft_tables(side):
    index = np.arange(side)
    angles = (index[:, None] * index[None, :] % side) * (2.0 * math.pi / side)
    cosine, sine = np.cos(angles), np.sin(angles)
    table = np.concatenate(
        [
            np.concatenate([cosine, sine], 1),
            np.concatenate([cosine, -sine], 1),
            np.concatenate([-sine, -cosine], 1),
        ],
        0,
    )
    high = table.astype(jnp.bfloat16)
    low = (table - high.astype(np.float64)).astype(jnp.bfloat16)
    return np.stack([high, low])


def dot(a, b):
    return jnp.dot(a, b, preferred_element_type=jnp.float32)


def split(a):
    high = a.astype(jnp.bfloat16)
    return high, (a - high.astype(jnp.float32)).astype(jnp.bfloat16)


def dot3(a, b):
    return dot(a[0], b[0]) + (dot(a[0], b[1]) + dot(a[1], b[0]))


def total(terms):
    terms = list(terms)
    while len(terms) > 1:
        terms = [
            terms[i] + terms[i + 1] if i + 1 < len(terms) else terms[i]
            for i in range(0, len(terms), 2)
        ]
    return terms[0]


def take(x, index):
    return jnp.take_along_axis(x, index, axis=1)


def row_chunks(row_count):
    cuts = [16] + list(range(32, row_count, 32)) + [row_count]
    return [(a, b) for a, b in zip(cuts[:-1], cuts[1:])] + [(0, 16)]


def load_pieces(row_count):
    cuts = [0, 32, 80, row_count - 8]
    return [(row_count - 8, row_count)] + [(a, b) for a, b in zip(cuts[:-1], cuts[1:])]


def forward(patch, tables):
    wide = tables[0, 0:PATCH, :], tables[1, 0:PATCH, :]
    square = tables[0, PATCH : 3 * PATCH, :], tables[1, PATCH : 3 * PATCH, :]
    first = dot(patch, wide[0]) + dot(patch, wide[1])
    stacked = jnp.concatenate([first[:, :PATCH], first[:, PATCH:]], 0)
    return dot3(square, split(stacked))


def surface(now, after, tables):
    wide = tables[0, 0:PATCH, :]
    square = tables[0, PATCH : 3 * PATCH, :]
    now_real, now_imag = now[0:PATCH], now[PATCH : 2 * PATCH]
    next_real, next_imag = after[0:PATCH], after[PATCH : 2 * PATCH]
    cross_real = now_real * next_real + now_imag * next_imag
    cross_imag = now_imag * next_real - now_real * next_imag
    magnitude = jnp.sqrt(cross_real * cross_real + cross_imag * cross_imag)
    mean = jnp.sum(jnp.sum(magnitude, axis=0, keepdims=True), axis=1, keepdims=True) * (
        1.0 / (PATCH * PATCH)
    )
    scaled = 1.0 / (magnitude + (0.5 * mean + 1e-06))
    damped = jnp.concatenate([cross_real * scaled, cross_imag * scaled], 1)
    back = dot(damped.astype(jnp.bfloat16), square)
    stacked = jnp.concatenate([back[:, :PATCH], back[:, PATCH:]], 0)
    return dot(wide, stacked.astype(jnp.bfloat16)) * (1.0 / PATCH)


def kernel(
    sizes,
    pixels,
    delays_hbm,
    drifts_hbm,
    weights_hbm,
    columns_hbm,
    tables_hbm,
    jitter_out,
    freq_out,
    early_out,
    tables,
    raw,
    delays,
    drifts,
    weights,
    columns,
    delay_rows,
    aligned,
    ahead,
    cross_sums,
    energies,
    jitter_rows,
    halo_out,
    halo_in,
    outbox,
    arrived,
    coefs,
    partial,
    patch_out,
    patch_in,
    freq,
    load_sem,
    table_sem,
    small_sem,
    halo_sem,
    block_send,
    block_recv,
    patch_send,
    patch_recv,
):
    sections, tiles, rows_axis, row_count, row_width, moves = sizes
    owners = tiles * rows_axis
    blocks = row_width // LANES
    per_seg = SEG // LANES
    segs = row_width // SEG
    slab_blocks = blocks // sections
    chunks = row_chunks(row_count)
    pieces = load_pieces(row_count)
    f32, bf16 = jnp.float32, jnp.bfloat16
    tile, row_at = lax.axis_index("tile"), lax.axis_index("row")
    me = tile * rows_axis + row_at
    section = lax.axis_index("sec")

    def band_device(band):
        return {"tile": band // rows_axis, "row": band % rows_axis}

    band_steps = [(t, r) for t in range(tiles) for r in range(rows_axis)][1:]
    band_steps.sort(key=lambda step: -min(step[0], tiles - step[0]))

    def slot_of(step):
        return step[0] * rows_axis + step[1] - 1

    def band_at(step):
        return (tile + step[0]) % tiles * rows_axis + (row_at + step[1]) % rows_axis

    def band_from(step):
        return (tile - step[0] + tiles) % tiles * rows_axis + (
            row_at - step[1] + rows_axis
        ) % rows_axis

    upper = 2 * section // sections
    targets = []
    for i in range(sections - 1):
        up = i + (i + sections - section) // sections
        down = sections - 1 - i
        down = down - 1 + (down + sections - section - 1) // sections
        targets.append(upper * up + (1 - upper) * down)
    targets.append(section)

    table_copy = pltpu.make_async_copy(tables_hbm, tables, table_sem)
    loads = [
        pltpu.make_async_copy(
            pixels.at[0, pl.ds(a, b - a)], raw.at[pl.ds(a, b - a)], load_sem.at[i]
        )
        for i, (a, b) in enumerate(pieces)
    ]
    small_copies = [
        pltpu.make_async_copy(source, target, small_sem.at[i])
        for i, (source, target) in enumerate(
            (
                (delays_hbm, delays),
                (drifts_hbm, drifts),
                (weights_hbm, weights),
                (columns_hbm, columns),
            )
        )
    ]
    small_copies[0].start()
    for copy in loads[:2]:
        copy.start()
    for copy in small_copies[1:]:
        copy.start()
    for copy in loads[2:]:
        copy.start()
    table_copy.start()

    barrier = pltpu.get_barrier_semaphore()
    for step in range(1, owners):
        pl.semaphore_signal(
            barrier, inc=1, device_id=band_device((me + step) % owners), device_id_type=MESH
        )
    for step in range(1, sections):
        pl.semaphore_signal(
            barrier, inc=1, device_id={"sec": (section + step) % sections}, device_id_type=MESH
        )

    lane = lax.broadcasted_iota(jnp.int32, (8, LANES), 1)
    first_lane, last_lane = lane == 0, lane == LANES - 1
    to_right, to_left = (lane + 1) & (LANES - 1), (lane + LANES - 1) & (LANES - 1)
    zero = jnp.zeros((8, LANES), f32)
    for g in range(0, row_count + 8, 8):
        aligned[0, g : g + 8, :] = zero
        aligned[blocks + 1, g : g + 8, :] = zero
    small_copies[0].wait()
    delay_rows[...] = (
        jnp.broadcast_to(delays[...].astype(f32), (LANES, row_count)).T
    ).astype(jnp.int32)

    def shifted(g):
        start = g * 8
        delay = delay_rows[start : start + 8, :]
        values = [raw[start : start + 8, v * LANES : (v + 1) * LANES] for v in range(blocks)]
        near = lane + delay
        here = [take(x, near & (LANES - 1)) for x in values] + [zero]
        far = near + 1
        there = [take(x, far & (LANES - 1)) for x in values] + [zero]
        near_kept, far_kept = near < LANES, far < LANES
        now, after = [], []
        for v in range(blocks):
            now.append(jnp.where(near_kept, here[v], here[v + 1]))
            x = jnp.where(far_kept, there[v], there[v + 1])
            if v % per_seg == per_seg - 1:
                x = jnp.where(last_lane, there[v + 1 - per_seg], x)
            after.append(x)
        return now, after

    def keep(g, now, after):
        rows = slice(g * 8 + 8, g * 8 + 16)
        for v in range(blocks):
            aligned[v + 1, rows, :] = now[v]
            ahead[v, rows, :] = after[v]
        energies[rows, :] = total(x * x for x in now)

    def compare(g, now=None, after=None):
        start = g * 8
        terms = []
        for v in range(blocks):
            x = now[v] if now else aligned[v + 1, start + 8 : start + 16, :]
            x_after = after[v] if after else ahead[v, start + 8 : start + 16, :]
            above = aligned[v + 1, start + 7 : start + 15, :]
            above_after = ahead[v, start + 7 : start + 15, :]
            terms.append(above * x_after - above_after * x)
        cross_sums[start : start + 8, :] = total(terms)

    halo = pltpu.make_async_remote_copy(
        src_ref=halo_out.at[:, pl.ds(7, 1)],
        dst_ref=halo_in,
        send_sem=halo_sem.at[0],
        recv_sem=halo_sem.at[1],
        device_id=band_device((me + 1) % owners),
        device_id_type=MESH,
    )
    for copy in small_copies[1:]:
        copy.wait()

    def pick(hits, values, default):
        first = second = default
        for hit, value in zip(hits[::-1], values[::-1]):
            second = jnp.where(hit, first, second)
            first = jnp.where(hit, value, first)
        return first, second

    own_sources = [drifts[0, 0, me, k] for k in range(moves)]
    own_owners = [drifts[0, 1, me, k] for k in range(moves)]
    sources = {}
    for step in band_steps + [(0, 0)]:
        owner = band_at(step)
        picked = pick([o == owner for o in own_owners], own_sources, jnp.int32(0))
        for rank in range(CAP):
            sources[step, rank] = picked[rank]

    def corrected(block, start):
        rows = slice(start + 8, start + 16)
        before, x, after = [aligned[block + i, rows, :] for i in range(3)]
        left = take(jnp.where(last_lane, before, x), to_left)
        right = take(jnp.where(first_lane, after, x), to_right)
        return x - jitter_rows[start : start + 8, :] * (right - left)

    def finish(a, b):
        numerator = jnp.sum(cross_sums[a:b, :], axis=1, keepdims=True) * (-0.5 / segs)
        power = energies[a + 8 : b + 8, :] + energies[a + 7 : b + 7, :]
        power = jnp.sum(power, axis=1, keepdims=True) * (0.5 / segs)
        jitter = jnp.broadcast_to(numerator / (power + 1e-05), (b - a, LANES))
        jitter_rows[a:b, :] = 0.5 * jitter

    def fill_blocks(c):
        a, b = chunks[c]
        for step in band_steps:
            for rank in range(CAP):
                for start in range(a, b, 16):
                    pair = [corrected(sources[step, rank], start + i) for i in (0, 8)]
                    outbox[slot_of(step), rank, start : start + 16, :] = jnp.concatenate(
                        pair, 0
                    ).astype(bf16)

    def send_blocks(c):
        a, b = chunks[c]
        for step in band_steps:
            slot = slot_of(step)
            copy = pltpu.make_async_remote_copy(
                src_ref=outbox.at[slot, :, pl.ds(a, b - a)],
                dst_ref=arrived.at[slot, :, pl.ds(a, b - a)],
                send_sem=block_send,
                recv_sem=block_recv.at[c],
                device_id=band_device(band_at(step)),
                device_id_type=MESH,
            )
            copy.start()

    steps = [(0, 0)] + band_steps
    keys = [(step, rank) for step in steps for rank in range(CAP)]

    offsets = [columns[0, target] for target in targets]
    blocks_at = [t * slab_blocks + o // LANES for t, o in zip(targets, offsets)]
    starts = [o % LANES for o in offsets]

    def weigh():
        found = {}
        for step in steps:
            band = band_from(step)
            hits = [drifts[0, 1, band, k] == me for k in range(moves)]
            picked = pick(hits, [drifts[0, 2, band, k] for k in range(moves)], jnp.int32(-1))
            heavy = pick(hits, [weights[0, band, k] for k in range(moves)], jnp.float32(0.0))
            for rank in range(CAP):
                found[step, rank] = picked[rank], heavy[rank]
        for p in range(sections):
            under = jnp.where(lane >= starts[p], blocks_at[p], blocks_at[p] + 1)
            shares = [jnp.where(under == found[key][0], found[key][1], 0.0) for key in keys]
            scale = 1.0 / (1.0 + total(shares))
            coefs[p, len(keys)] = scale
            for i, share in enumerate(shares):
                coefs[p, i] = share * scale

    def own_part(a, b):
        for start in range(a, b, 8):
            rows = slice(start + 8, start + 16)
            half = jitter_rows[start : start + 8, :]
            mine = [
                corrected(sources[(0, 0), rank], start).astype(bf16).astype(f32)
                for rank in range(CAP)
            ]
            for p in range(sections):
                block, offset = blocks_at[p], starts[p]
                before, x, after = [aligned[block + i, rows, :] for i in range(3)]
                left = jnp.where(lane >= offset - 1, x, after)
                left = jnp.where((lane - offset) == LANES - 1, before, left)
                left = take(left, to_left)
                right = take(jnp.where(lane > offset, x, after), to_right)
                value = jnp.where(lane >= offset, x, after) - half * (right - left)
                value = value.astype(bf16).astype(f32) * coefs[p, len(keys)]
                for rank in range(CAP):
                    value = value + coefs[p, rank] * mine[rank]
                partial[p, start : start + 8, :] = value

    def send_patches(c):
        a, b = chunks[c]
        pltpu.make_async_copy(
            arrived.at[:, :, pl.ds(a, b - a)], arrived.at[:, :, pl.ds(a, b - a)], block_recv.at[c]
        ).wait()
        for start in range(a, b, 16):
            blocks_in = [
                arrived[slot_of(step), rank, start : start + 16, :].astype(f32)
                for step, rank in keys[CAP:]
            ]
            for p in range(sections):
                turn = (lane + starts[p]) & (LANES - 1)
                shares = [coefs[p, CAP + i] for i in range(len(blocks_in))]
                values = []
                for i in (0, 8):
                    terms = [share * x[i : i + 8] for share, x in zip(shares, blocks_in)]
                    values.append(take(partial[p, start + i : start + i + 8, :] + total(terms), turn))
                patch = jnp.concatenate(values, 0).astype(bf16)
                if p < sections - 1:
                    patch_out[p, start : start + 16, :] = patch
                else:
                    patch_in[section, start : start + 16, :] = patch
        for p, target in enumerate(targets[:-1]):
            pltpu.make_async_remote_copy(
                src_ref=patch_out.at[p, pl.ds(a, b - a)],
                dst_ref=patch_in.at[section, pl.ds(a, b - a)],
                send_sem=patch_send,
                recv_sem=patch_recv.at[section],
                device_id={"sec": target},
                device_id_type=MESH,
            ).start()

    last_group = row_count // 8 - 1

    def group(g):
        if g == last_group:
            compare(g)
            return
        now, after = shifted(g)
        keep(g, now, after)
        compare(g, now, after)

    loads[0].wait()
    loads[1].wait()
    keep(last_group, *shifted(last_group))
    for v in range(blocks):
        halo_out[v, :, :] = aligned[v + 1, row_count : row_count + 8, :]
    keep(1, *shifted(1))
    for c, (a, b) in enumerate(chunks[:-1]):
        if c == 1:
            for load in loads[2:]:
                load.wait()
        for g in range(a // 8, b // 8):
            group(g)
        finish(a, b)
        fill_blocks(c)
        if c == 0:
            pl.semaphore_wait(barrier, owners + sections - 2)
            halo.start()
        send_blocks(c)

    keep(0, *shifted(0))
    compare(1)
    halo.wait_recv()
    shown = jnp.where(me == 0, 0.0, 1.0)
    above = [shown * jnp.broadcast_to(halo_in[v], (8, LANES)) for v in range(blocks)]
    turned = [take(x, to_right) for x in above]
    for v in range(blocks):
        follows = v + 1 - per_seg if v % per_seg == per_seg - 1 else v + 1
        aligned[v + 1, 0:8, :] = above[v]
        ahead[v, 0:8, :] = jnp.where(last_lane, turned[follows], turned[v])
    energies[0:8, :] = total(x * x for x in above)
    compare(0)
    finish(*chunks[-1])
    fill_blocks(len(chunks) - 1)
    send_blocks(len(chunks) - 1)
    weigh()
    for a, b in chunks:
        own_part(a, b)
    for c in range(len(chunks)):
        send_patches(c)

    jitter_out[...] = 2.0 * jitter_rows[...].T[0:1, :]
    table_copy.wait()
    for s in range(sections):

        @pl.when(section != s)
        def _():
            pltpu.make_async_copy(patch_in.at[s], patch_in.at[s], patch_recv.at[s]).wait()

        if s < sections - 2:
            freq[s] = forward(patch_in[s], tables)
        else:
            freq_out[s - sections + 2] = forward(patch_in[s], tables)
        if 0 < s < sections - 1:
            after = freq[s] if s < sections - 2 else freq_out[0]
            early_out[s - 1] = surface(freq[s - 1], after, tables)

    halo.wait_send()
    pltpu.make_async_copy(outbox, outbox, block_send).wait()
    pltpu.make_async_copy(patch_out, patch_out, patch_send).wait()


def correlate(freq, tables, jitter, early, jitter_out, surfaces_out, late, sem):
    pairs = early.shape[0]
    copies = [
        pltpu.make_async_copy(early, surfaces_out.at[pl.ds(0, pairs), 0, 0], sem.at[0]),
        pltpu.make_async_copy(jitter, jitter_out, sem.at[1]),
        pltpu.make_async_copy(late, surfaces_out.at[pairs, 0, 0], sem.at[2]),
    ]
    copies[0].start()
    copies[1].start()
    late[...] = surface(freq[0], freq[1], tables)
    copies[2].start()
    for copy in copies:
        copy.wait()


def per_device(section_pixels, jitter_index, drift_list, blend_weight, patch_col):
    _, row_count, row_width = section_pixels.shape
    sections = lax.axis_size("sec")
    tiles, rows_axis = lax.axis_size("tile"), lax.axis_size("row")
    owners = tiles * rows_axis
    moves = drift_list.shape[2]
    blocks = row_width // LANES
    chunks = len(row_chunks(row_count))
    pieces = len(load_pieces(row_count))
    sizes = (sections, tiles, rows_axis, row_count, row_width, moves)
    tables = dft_tables(PATCH)
    f32, bf16 = jnp.float32, jnp.bfloat16
    vmem = pl.BlockSpec(memory_space=pltpu.VMEM)
    anywhere = pl.BlockSpec(memory_space=pl.ANY)
    dma = pltpu.SemaphoreType.DMA
    between = pl.pallas_call(
        functools.partial(kernel, sizes),
        out_shape=(
            pltpu.VMEM((1, row_count), f32),
            pltpu.VMEM((2, 2 * PATCH, PATCH), f32),
            pltpu.VMEM((sections - 2, PATCH, PATCH), f32),
            pltpu.VMEM(tables.shape, bf16),
        ),
        in_specs=[anywhere] * 6,
        out_specs=(vmem,) * 4,
        scratch_shapes=[
            pltpu.VMEM((row_count, row_width), f32),
            pltpu.VMEM(jitter_index.shape, jnp.int32),
            pltpu.SMEM((1, 3, owners, moves), jnp.int32),
            pltpu.SMEM(blend_weight.shape, f32),
            pltpu.SMEM(patch_col.shape, jnp.int32),
            pltpu.VMEM((row_count, LANES), jnp.int32),
            pltpu.VMEM((blocks + 2, row_count + 8, LANES), f32),
            pltpu.VMEM((blocks, row_count + 8, LANES), f32),
            pltpu.VMEM((row_count, LANES), f32),
            pltpu.VMEM((row_count + 8, LANES), f32),
            pltpu.VMEM((row_count, LANES), f32),
            pltpu.VMEM((blocks, 8, LANES), f32),
            pltpu.VMEM((blocks, 1, LANES), f32),
            pltpu.VMEM((owners - 1, CAP, BLOCK, BLOCK), bf16),
            pltpu.VMEM((owners - 1, CAP, BLOCK, BLOCK), bf16),
            pltpu.VMEM((sections, owners * CAP + 1, 8, LANES), f32),
            pltpu.VMEM((sections, PATCH, LANES), f32),
            pltpu.VMEM((sections - 1, PATCH, PATCH), bf16),
            pltpu.VMEM((sections, PATCH, PATCH), bf16),
            pltpu.VMEM((sections - 2, 2 * PATCH, PATCH), f32),
            dma((pieces,)),
            dma,
            dma((4,)),
            dma((2,)),
            dma,
            dma((chunks,)),
            dma,
            dma((sections,)),
        ],
        compiler_params=pltpu.CompilerParams(collective_id=0, has_side_effects=True),
        name="section_patches",
    )(
        section_pixels,
        jitter_index,
        jnp.transpose(drift_list, (0, 3, 1, 2)),
        blend_weight,
        patch_col,
        tables,
    )
    jitter, freq, early, tables = [
        pltpu.with_memory_space_constraint(x, pltpu.VMEM) for x in between
    ]
    return pl.pallas_call(
        correlate,
        out_shape=(
            jax.ShapeDtypeStruct((1, row_count), f32),
            jax.ShapeDtypeStruct((sections - 1, 1, 1, PATCH, PATCH), f32),
        ),
        in_specs=[vmem] * 4,
        out_specs=(anywhere, anywhere),
        scratch_shapes=[pltpu.VMEM((PATCH, PATCH), f32), dma((3,))],
        name="section_correlation",
    )(freq, tables, jitter, early)


def solution(mesh):
    in_specs = (
        P(("groups", "sec"), ("tile", "row"), None),
        P(("groups", "sec"), ("tile", "row")),
        P(("groups", "sec"), None, None, None),
        P(("groups", "sec"), None, None),
        P(("tile", "row"), "groups"),
    )
    out_specs = (
        P(("groups", "sec"), ("tile", "row")),
        P("groups", ("tile", "row"), "sec", None, None),
    )
    return jax.shard_map(
        per_device, mesh=mesh, in_specs=in_specs, out_specs=out_specs, check_vma=False
    )
```

time: 19.1 us -> 17.1 us (0.90)
  Pallas kernels: 18.3 us -> 16.3 us
    pallas_call x1, Pallas kernels: 17 us -> 15.2 us  [per_device(): pl.pallas_call(functools.partial(kernel, sizes), out_shape=(pltpu.VMEM((1...]
    pallas_call x1, Pallas kernels: 1.34 us -> 1.1 us  [per_device(): pl.pallas_call(correlate, out_shape=(jax.ShapeDtypeStruct((1, row_count),...]
where the time goes in v1:
time: 17.1 us; the launch traced here: 17 us
  Pallas kernels  16.3 us (95%)
  between operations  0.64 us (4%)
    pallas_call x1, Pallas kernels, per_device(): pl.pallas_call(functools.partial(kernel, sizes), out_shape=(pltpu.VMEM((1...  15.2 us
    pallas_call x1, Pallas kernels, per_device(): pl.pallas_call(correlate, out_shape=(jax.ShapeDtypeStruct((1, row_count),...  1.1 us

profile of v1, /device:TPU:0, one launch (start us, length us, event | category | flops | bytes accessed | tf_op | source)
XLA Modules:
  0.0 17.0 jit_solution(11317030869908675691)
XLA Ops:
  0.6 15.2 %section_patches.1 = (f32[1,128]{1,0:T(1,128)S(1)}, f32[2,256,128]{2,1,0:T(8,128)S(1)}, f32[2,128,128]{2,1,0:T(8,128)S(1)}, bf16[2,384,256]{2,1,0:T(8,128)(2,1)S(1)}) custom-call(f32[1,128,4096]{2,1,0:T(8,128)} %pixels.1, s32[1,128]{1,0:T(1,128)} %delays_hbm.1, s32[1,3,4,8]{3,2,1,0:T(4,128)} %bitcast.1, f32[1,4,8]{2,1,0:T(4,128)} %weights_hbm.1, ...), custom_call_target="tpu_custom_call" | custom-call | tf_op jit(solution)/shard_map/section_patches/pallas_call | solution.py:508
  15.9 1.1 %section_correlation.1 = (f32[1,128]{1,0:T(1,128)}, f32[3,1,1,128,128]{4,3,2,1,0:T(8,128)}) custom-call(f32[2,256,128]{2,1,0:T(8,128)S(1)} %get-tuple-element.6.freq, bf16[2,384,256]{2,1,0:T(8,128)(2,1)S(1)} %get-tuple-element.7.tables, f32[1,128]{1,0:T(1,128)S(1)} %get-tuple-element.8.jitter, f32[2,128,128]{2,1,0:T(8,128)S(1)} %get-tuple-element.9.early), custom_call_target="tpu_custom_call" | custom-call | tf_op jit(solution)/shard_map/section_correlation/pallas_call | solution.py:561

commit v2 on v1

--- a/solution.py
+++ b/solution.py
@@ -62,13 +62,13 @@
 
 
 def row_chunks(row_count):
-    cuts = [16] + list(range(32, row_count, 32)) + [row_count]
-    return [(a, b) for a, b in zip(cuts[:-1], cuts[1:])] + [(0, 16)]
+    cuts = [0, 16] + list(range(48, row_count - 16, 32)) + [row_count - 16, row_count]
+    return [(a, b) for a, b in zip(cuts[:-1], cuts[1:])][::-1]
 
 
 def load_pieces(row_count):
-    cuts = [0, 32, 80, row_count - 8]
-    return [(row_count - 8, row_count)] + [(a, b) for a, b in zip(cuts[:-1], cuts[1:])]
+    cuts = [max(a - 8, 0) for a, _ in row_chunks(row_count)]
+    return [(a, b) for a, b in zip(cuts[:-2] + [0], [row_count] + cuts[:-2])]
 
 
 def forward(patch, tables):
@@ -196,11 +196,10 @@
         )
     ]
     small_copies[0].start()
-    for copy in loads[:2]:
-        copy.start()
+    loads[0].start()
     for copy in small_copies[1:]:
         copy.start()
-    for copy in loads[2:]:
+    for copy in loads[1:]:
         copy.start()
     table_copy.start()
 
@@ -270,8 +269,6 @@
         device_id=band_device((me + 1) % owners),
         device_id_type=MESH,
     )
-    for copy in small_copies[1:]:
-        copy.wait()
 
     def pick(hits, values, default):
         first = second = default
@@ -280,14 +277,18 @@
             first = jnp.where(hit, value, first)
         return first, second
 
-    own_sources = [drifts[0, 0, me, k] for k in range(moves)]
-    own_owners = [drifts[0, 1, me, k] for k in range(moves)]
     sources = {}
-    for step in band_steps + [(0, 0)]:
-        owner = band_at(step)
-        picked = pick([o == owner for o in own_owners], own_sources, jnp.int32(0))
-        for rank in range(CAP):
-            sources[step, rank] = picked[rank]
+
+    def find_sources():
+        own_sources = [drifts[0, 0, me, k] for k in range(moves)]
+        own_owners = [drifts[0, 1, me, k] for k in range(moves)]
+        found = {}
+        for step in band_steps + [(0, 0)]:
+            owner = band_at(step)
+            picked = pick([o == owner for o in own_owners], own_sources, jnp.int32(0))
+            for rank in range(CAP):
+                found[step, rank] = picked[rank]
+        return found
 
     def corrected(block, start):
         rows = slice(start + 8, start + 16)
@@ -330,11 +331,13 @@
     steps = [(0, 0)] + band_steps
     keys = [(step, rank) for step in steps for rank in range(CAP)]
 
-    offsets = [columns[0, target] for target in targets]
-    blocks_at = [t * slab_blocks + o // LANES for t, o in zip(targets, offsets)]
-    starts = [o % LANES for o in offsets]
+    blocks_at, starts = [], []
 
     def weigh():
+        for target in targets:
+            offset = columns[0, target]
+            blocks_at.append(target * slab_blocks + offset // LANES)
+            starts.append(offset % LANES)
         found = {}
         for step in steps:
             band = band_from(step)
@@ -404,54 +407,80 @@
                 device_id_type=MESH,
             ).start()
 
-    last_group = row_count // 8 - 1
+    aligned_groups = set()
 
     def group(g):
-        if g == last_group:
-            compare(g)
-            return
         now, after = shifted(g)
         keep(g, now, after)
-        compare(g, now, after)
-
+        aligned_groups.add(g)
+        return now, after
+
+    def above(c):
+        group(chunks[c][0] // 8 - 1)
+
+    def groups(c, part=None):
+        a, b = chunks[c][0] // 8, chunks[c][1] // 8
+        todo = list(range(a, b))
+        if part is not None:
+            half = (b - a) // 2 - 1
+            todo = todo[:half] if part == 0 else todo[half:]
+        for g in todo:
+            if g in aligned_groups:
+                compare(g)
+            else:
+                compare(g, *group(g))
+
+    def finish_and_fill(c):
+        finish(*chunks[c])
+        fill_blocks(c)
+
+    def halo_rows():
+        shown = jnp.where(me == 0, 0.0, 1.0)
+        rows = [shown * jnp.broadcast_to(halo_in[v], (8, LANES)) for v in range(blocks)]
+        turned = [take(x, to_right) for x in rows]
+        for v in range(blocks):
+            follows = v + 1 - per_seg if v % per_seg == per_seg - 1 else v + 1
+            aligned[v + 1, 0:8, :] = rows[v]
+            ahead[v, 0:8, :] = jnp.where(last_lane, turned[follows], turned[v])
+        energies[0:8, :] = total(x * x for x in rows)
+
+    last = len(chunks) - 1
     loads[0].wait()
-    loads[1].wait()
-    keep(last_group, *shifted(last_group))
+    for copy in small_copies[1:]:
+        copy.wait()
+    sources.update(find_sources())
+    above(0)
+    groups(0)
     for v in range(blocks):
         halo_out[v, :, :] = aligned[v + 1, row_count : row_count + 8, :]
-    keep(1, *shifted(1))
-    for c, (a, b) in enumerate(chunks[:-1]):
-        if c == 1:
-            for load in loads[2:]:
-                load.wait()
-        for g in range(a // 8, b // 8):
-            group(g)
-        finish(a, b)
-        fill_blocks(c)
-        if c == 0:
-            pl.semaphore_wait(barrier, owners + sections - 2)
-            halo.start()
+    finish_and_fill(0)
+    pl.semaphore_wait(barrier, owners + sections - 2)
+    send_blocks(0)
+    halo.start()
+    for load in loads[1:]:
+        load.wait()
+    weigh()
+    above(1)
+    groups(1)
+    for c in range(1, last):
+        finish_and_fill(c)
+        if c < last - 1:
+            above(c + 1)
+            groups(c + 1, 0)
+        else:
+            group(0)
+            own_part(*chunks[0])
         send_blocks(c)
-
-    keep(0, *shifted(0))
-    compare(1)
+        if c < last - 1:
+            groups(c + 1, 1)
     halo.wait_recv()
-    shown = jnp.where(me == 0, 0.0, 1.0)
-    above = [shown * jnp.broadcast_to(halo_in[v], (8, LANES)) for v in range(blocks)]
-    turned = [take(x, to_right) for x in above]
-    for v in range(blocks):
-        follows = v + 1 - per_seg if v % per_seg == per_seg - 1 else v + 1
-        aligned[v + 1, 0:8, :] = above[v]
-        ahead[v, 0:8, :] = jnp.where(last_lane, turned[follows], turned[v])
-    energies[0:8, :] = total(x * x for x in above)
-    compare(0)
-    finish(*chunks[-1])
-    fill_blocks(len(chunks) - 1)
-    send_blocks(len(chunks) - 1)
-    weigh()
-    for a, b in chunks:
-        own_part(a, b)
-    for c in range(len(chunks)):
+    halo_rows()
+    groups(last)
+    finish_and_fill(last)
+    send_blocks(last)
+    for c in range(1, last + 1):
+        own_part(*chunks[c])
+    for c in range(last + 1):
         send_patches(c)
 
     jitter_out[...] = 2.0 * jitter_rows[...].T[0:1, :]
@@ -462,13 +491,12 @@
         def _():
             pltpu.make_async_copy(patch_in.at[s], patch_in.at[s], patch_recv.at[s]).wait()
 
-        if s < sections - 2:
-            freq[s] = forward(patch_in[s], tables)
-        else:
-            freq_out[s - sections + 2] = forward(patch_in[s], tables)
-        if 0 < s < sections - 1:
-            after = freq[s] if s < sections - 2 else freq_out[0]
-            early_out[s - 1] = surface(freq[s - 1], after, tables)
+        if s > 1:
+            early_out[s - 2] = surface(freq[s - 2], freq[s - 1], tables)
+        spectrum = forward(patch_in[s], tables)
+        freq[s] = spectrum
+        if s > sections - 3:
+            freq_out[s - sections + 2] = spectrum
 
     halo.wait_send()
     pltpu.make_async_copy(outbox, outbox, block_send).wait()
@@ -535,7 +563,7 @@
             pltpu.VMEM((sections, PATCH, LANES), f32),
             pltpu.VMEM((sections - 1, PATCH, PATCH), bf16),
             pltpu.VMEM((sections, PATCH, PATCH), bf16),
-            pltpu.VMEM((sections - 2, 2 * PATCH, PATCH), f32),
+            pltpu.VMEM((sections, 2 * PATCH, PATCH), f32),
             dma((pieces,)),
             dma,
             dma((4,)),

time: 17.1 us -> 16.8 us (0.982)
  Pallas kernels: 16.3 us -> 16 us
    pallas_call x1, Pallas kernels: 15.2 us -> 14.9 us  [per_device(): pl.pallas_call(functools.partial(kernel, sizes), out_shape=(pltpu.VMEM((1...]
where the time goes in v2:
time: 16.8 us; the launch traced here: 16.6 us
  Pallas kernels  16 us (95%)
  between operations  0.64 us (4%)
    pallas_call x1, Pallas kernels, per_device(): pl.pallas_call(functools.partial(kernel, sizes), out_shape=(pltpu.VMEM((1...  14.9 us
    pallas_call x1, Pallas kernels, per_device(): pl.pallas_call(correlate, out_shape=(jax.ShapeDtypeStruct((1, row_count),...  1.1 us

profile of v2, /device:TPU:0, one launch (start us, length us, event | category | flops | bytes accessed | tf_op | source)
XLA Modules:
  0.0 16.6 jit_solution(11215515679886548168)
XLA Ops:
  0.6 14.9 %section_patches.1 = (f32[1,128]{1,0:T(1,128)S(1)}, f32[2,256,128]{2,1,0:T(8,128)S(1)}, f32[2,128,128]{2,1,0:T(8,128)S(1)}, bf16[2,384,256]{2,1,0:T(8,128)(2,1)S(1)}) custom-call(f32[1,128,4096]{2,1,0:T(8,128)} %pixels.1, s32[1,128]{1,0:T(1,128)} %delays_hbm.1, s32[1,3,4,8]{3,2,1,0:T(4,128)} %bitcast.1, f32[1,4,8]{2,1,0:T(4,128)} %weights_hbm.1, ...), custom_call_target="tpu_custom_call" | custom-call | tf_op jit(solution)/shard_map/section_patches/pallas_call | solution.py:536
  15.5 1.1 %section_correlation.1 = (f32[1,128]{1,0:T(1,128)}, f32[3,1,1,128,128]{4,3,2,1,0:T(8,128)}) custom-call(f32[2,256,128]{2,1,0:T(8,128)S(1)} %get-tuple-element.6.freq, bf16[2,384,256]{2,1,0:T(8,128)(2,1)S(1)} %get-tuple-element.7.tables, f32[1,128]{1,0:T(1,128)S(1)} %get-tuple-element.8.jitter, f32[2,128,128]{2,1,0:T(8,128)S(1)} %get-tuple-element.9.early), custom_call_target="tpu_custom_call" | custom-call | tf_op jit(solution)/shard_map/section_correlation/pallas_call | solution.py:589

commit v3 on v2

--- a/solution.py
+++ b/solution.py
@@ -67,8 +67,12 @@
 
 
 def load_pieces(row_count):
-    cuts = [max(a - 8, 0) for a, _ in row_chunks(row_count)]
-    return [(a, b) for a, b in zip(cuts[:-2] + [0], [row_count] + cuts[:-2])]
+    cuts = [row_count] + list(range(row_count - 24, 0, -32))
+    return [(a, b) for a, b in zip(cuts[1:-1] + [0], cuts[:-1])]
+
+
+def downward(section, sections):
+    return (section + sections - 1) // sections
 
 
 def forward(patch, tables):
@@ -124,8 +128,11 @@
     halo_in,
     outbox,
     arrived,
+    spots_out,
+    spots_in,
+    base_out,
+    base_in,
     coefs,
-    partial,
     patch_out,
     patch_in,
     freq,
@@ -135,6 +142,8 @@
     halo_sem,
     block_send,
     block_recv,
+    side_send,
+    side_recv,
     patch_send,
     patch_recv,
 ):
@@ -154,28 +163,17 @@
     def band_device(band):
         return {"tile": band // rows_axis, "row": band % rows_axis}
 
-    band_steps = [(t, r) for t in range(tiles) for r in range(rows_axis)][1:]
-    band_steps.sort(key=lambda step: -min(step[0], tiles - step[0]))
-
-    def slot_of(step):
-        return step[0] * rows_axis + step[1] - 1
-
-    def band_at(step):
-        return (tile + step[0]) % tiles * rows_axis + (row_at + step[1]) % rows_axis
-
-    def band_from(step):
-        return (tile - step[0] + tiles) % tiles * rows_axis + (
-            row_at - step[1] + rows_axis
-        ) % rows_axis
-
-    upper = 2 * section // sections
-    targets = []
-    for i in range(sections - 1):
-        up = i + (i + sections - section) // sections
-        down = sections - 1 - i
-        down = down - 1 + (down + sections - section - 1) // sections
-        targets.append(upper * up + (1 - upper) * down)
-    targets.append(section)
+    blends = row_at == rows_axis - 1
+    others = [i + (i + owners - me) // owners for i in range(owners - 1)]
+
+    def tile_at(step):
+        return (tile + step) % tiles
+
+    def blender(at):
+        return {"tile": at, "row": rows_axis - 1}
+
+    def place_at(at):
+        return me - (me - (at + 1) * rows_axis + owners) // owners
 
     table_copy = pltpu.make_async_copy(tables_hbm, tables, table_sem)
     loads = [
@@ -197,21 +195,27 @@
     ]
     small_copies[0].start()
     loads[0].start()
-    for copy in small_copies[1:]:
+    barrier = pltpu.get_barrier_semaphore()
+    for step in range(1, sections):
+        far = (section + step) % sections
+        pl.semaphore_signal(
+            barrier, inc=1, device_id={"sec": far, "row": rows_axis - 1}, device_id_type=MESH
+        )
+    for copy in small_copies[1:] + loads[1:2]:
         copy.start()
-    for copy in loads[1:]:
+    for band in others:
+        pl.semaphore_signal(barrier, inc=1, device_id=band_device(band), device_id_type=MESH)
+
+    @pl.when(blends)
+    def _():
+        for step in range(1, sections):
+            for r in range(rows_axis - 1):
+                far = {"sec": (section + step) % sections, "row": r}
+                pl.semaphore_signal(barrier, inc=1, device_id=far, device_id_type=MESH)
+
+    for copy in loads[2:]:
         copy.start()
     table_copy.start()
-
-    barrier = pltpu.get_barrier_semaphore()
-    for step in range(1, owners):
-        pl.semaphore_signal(
-            barrier, inc=1, device_id=band_device((me + step) % owners), device_id_type=MESH
-        )
-    for step in range(1, sections):
-        pl.semaphore_signal(
-            barrier, inc=1, device_id={"sec": (section + step) % sections}, device_id_type=MESH
-        )
 
     lane = lax.broadcasted_iota(jnp.int32, (8, LANES), 1)
     first_lane, last_lane = lane == 0, lane == LANES - 1
@@ -282,13 +286,12 @@
     def find_sources():
         own_sources = [drifts[0, 0, me, k] for k in range(moves)]
         own_owners = [drifts[0, 1, me, k] for k in range(moves)]
-        found = {}
-        for step in band_steps + [(0, 0)]:
-            owner = band_at(step)
-            picked = pick([o == owner for o in own_owners], own_sources, jnp.int32(0))
-            for rank in range(CAP):
-                found[step, rank] = picked[rank]
-        return found
+        for step in range(tiles):
+            for r in range(rows_axis):
+                band = tile_at(step) * rows_axis + r
+                picked = pick([o == band for o in own_owners], own_sources, jnp.int32(0))
+                for rank in range(CAP):
+                    sources[step, r, rank] = picked[rank]
 
     def corrected(block, start):
         rows = slice(start + 8, start + 16)
@@ -304,106 +307,125 @@
         jitter = jnp.broadcast_to(numerator / (power + 1e-05), (b - a, LANES))
         jitter_rows[a:b, :] = 0.5 * jitter
 
-    def fill_blocks(c):
+    def fill_blocks(step, r, c):
         a, b = chunks[c]
-        for step in band_steps:
-            for rank in range(CAP):
-                for start in range(a, b, 16):
-                    pair = [corrected(sources[step, rank], start + i) for i in (0, 8)]
-                    outbox[slot_of(step), rank, start : start + 16, :] = jnp.concatenate(
-                        pair, 0
-                    ).astype(bf16)
-
-    def send_blocks(c):
-        a, b = chunks[c]
-        for step in band_steps:
-            slot = slot_of(step)
-            copy = pltpu.make_async_remote_copy(
-                src_ref=outbox.at[slot, :, pl.ds(a, b - a)],
-                dst_ref=arrived.at[slot, :, pl.ds(a, b - a)],
-                send_sem=block_send,
-                recv_sem=block_recv.at[c],
-                device_id=band_device(band_at(step)),
-                device_id_type=MESH,
-            )
-            copy.start()
-
-    steps = [(0, 0)] + band_steps
-    keys = [(step, rank) for step in steps for rank in range(CAP)]
-
-    blocks_at, starts = [], []
-
-    def weigh():
-        for target in targets:
-            offset = columns[0, target]
-            blocks_at.append(target * slab_blocks + offset // LANES)
-            starts.append(offset % LANES)
+        for rank in range(CAP):
+            for start in range(a, b, 16):
+                block = sources[step, r, rank]
+                pair = [corrected(block, start + half) for half in (0, 8)]
+                outbox[step, r, rank, start : start + 16, :] = jnp.concatenate(pair, 0).astype(bf16)
+
+    def send_blocks(step, sent):
+        at = tile_at(step)
+
+        def start():
+            for r, c in sent:
+                a, b = chunks[c]
+                pltpu.make_async_remote_copy(
+                    src_ref=outbox.at[step, r, :, pl.ds(a, b - a)],
+                    dst_ref=arrived.at[r, place_at(at), :, pl.ds(a, b - a)],
+                    send_sem=block_send,
+                    recv_sem=block_recv.at[r, c],
+                    device_id=blender(at),
+                    device_id_type=MESH,
+                ).start()
+
+        if step:
+            start()
+        else:
+            pl.when(row_at != rows_axis - 1)(start)
+
+    def fill_base(patches):
+        for p in patches:
+            offset = columns[0, p] % LANES
+            block = p * slab_blocks + columns[0, p] // LANES
+            for start in range(0, row_count, 16):
+                pair = []
+                for at in (start, start + 8):
+                    rows = slice(at + 8, at + 16)
+                    before, x, after = [aligned[block + i, rows, :] for i in range(3)]
+                    left = jnp.where(lane >= offset - 1, x, after)
+                    left = jnp.where((lane - offset) == LANES - 1, before, left)
+                    left = take(left, to_left)
+                    right = take(jnp.where(lane > offset, x, after), to_right)
+                    half = jitter_rows[at : at + 8, :]
+                    pair.append(jnp.where(lane >= offset, x, after) - half * (right - left))
+                base_out[p, start : start + 16, :] = jnp.concatenate(pair, 0).astype(bf16)
+
+    def side_copy(source, target, i):
+        return pltpu.make_async_remote_copy(
+            src_ref=source,
+            dst_ref=target,
+            send_sem=side_send.at[i],
+            recv_sem=side_recv.at[i],
+            device_id=blender(tile),
+            device_id_type=MESH,
+        )
+
+    row_slot = row_at % max(rows_axis - 1, 1)
+    spots_copy = side_copy(spots_out, spots_in.at[row_slot], 0)
+    base_copies = [
+        side_copy(base_out.at[pl.ds(0, 1)], base_in.at[row_slot, pl.ds(0, 1)], 1),
+        side_copy(
+            base_out.at[pl.ds(1, sections - 1)], base_in.at[row_slot, pl.ds(1, sections - 1)], 2
+        ),
+    ]
+
+    keys = [(i, rank) for i in range(owners) for rank in range(CAP)]
+
+    def spot(r, p):
+        spots = spots_out if r == rows_axis - 1 else spots_in.at[r]
+        column = jnp.broadcast_to(spots[p : p + 1, :], (8, LANES)).astype(jnp.int32)
+        return column & (LANES - 1), p * slab_blocks + column // LANES
+
+    def weigh(r):
         found = {}
-        for step in steps:
-            band = band_from(step)
-            hits = [drifts[0, 1, band, k] == me for k in range(moves)]
+        owner = tile * rows_axis + r
+        for i, band in enumerate([me] + others):
+            hits = [drifts[0, 1, band, k] == owner for k in range(moves)]
             picked = pick(hits, [drifts[0, 2, band, k] for k in range(moves)], jnp.int32(-1))
             heavy = pick(hits, [weights[0, band, k] for k in range(moves)], jnp.float32(0.0))
             for rank in range(CAP):
-                found[step, rank] = picked[rank], heavy[rank]
+                found[i, rank] = picked[rank], heavy[rank]
         for p in range(sections):
-            under = jnp.where(lane >= starts[p], blocks_at[p], blocks_at[p] + 1)
+            first, block = spot(r, p)
+            under = jnp.where(lane >= first, block, block + 1)
             shares = [jnp.where(under == found[key][0], found[key][1], 0.0) for key in keys]
             scale = 1.0 / (1.0 + total(shares))
-            coefs[p, len(keys)] = scale
+            coefs[r, p, len(keys)] = scale
             for i, share in enumerate(shares):
-                coefs[p, i] = share * scale
-
-    def own_part(a, b):
-        for start in range(a, b, 8):
-            rows = slice(start + 8, start + 16)
-            half = jitter_rows[start : start + 8, :]
-            mine = [
-                corrected(sources[(0, 0), rank], start).astype(bf16).astype(f32)
-                for rank in range(CAP)
-            ]
-            for p in range(sections):
-                block, offset = blocks_at[p], starts[p]
-                before, x, after = [aligned[block + i, rows, :] for i in range(3)]
-                left = jnp.where(lane >= offset - 1, x, after)
-                left = jnp.where((lane - offset) == LANES - 1, before, left)
-                left = take(left, to_left)
-                right = take(jnp.where(lane > offset, x, after), to_right)
-                value = jnp.where(lane >= offset, x, after) - half * (right - left)
-                value = value.astype(bf16).astype(f32) * coefs[p, len(keys)]
-                for rank in range(CAP):
-                    value = value + coefs[p, rank] * mine[rank]
-                partial[p, start : start + 8, :] = value
-
-    def send_patches(c):
+                coefs[r, p, i] = share * scale
+
+    def wait_blocks(r, c):
         a, b = chunks[c]
-        pltpu.make_async_copy(
-            arrived.at[:, :, pl.ds(a, b - a)], arrived.at[:, :, pl.ds(a, b - a)], block_recv.at[c]
-        ).wait()
+        landed = arrived.at[r, :, :, pl.ds(a, b - a)]
+        pltpu.make_async_copy(landed, landed, block_recv.at[r, c]).wait()
+
+    def blend(r, patches, a, b):
+        turns = [(lane + spot(r, p)[0]) & (LANES - 1) for p in patches]
         for start in range(a, b, 16):
-            blocks_in = [
-                arrived[slot_of(step), rank, start : start + 16, :].astype(f32)
-                for step, rank in keys[CAP:]
-            ]
-            for p in range(sections):
-                turn = (lane + starts[p]) & (LANES - 1)
-                shares = [coefs[p, CAP + i] for i in range(len(blocks_in))]
+            rows = slice(start, start + 16)
+            moved = [outbox[0, r, rank, rows, :].astype(f32) for rank in range(CAP)]
+            moved += [arrived[r, i - 1, rank, rows, :].astype(f32) for i, rank in keys[CAP:]]
+            for p, turn in zip(patches, turns):
+                base = base_out[p, rows, :] if r == rows_axis - 1 else base_in[r, p, rows, :]
+                shares = [coefs[r, p, i] for i in range(len(keys) + 1)]
                 values = []
                 for i in (0, 8):
-                    terms = [share * x[i : i + 8] for share, x in zip(shares, blocks_in)]
-                    values.append(take(partial[p, start + i : start + i + 8, :] + total(terms), turn))
-                patch = jnp.concatenate(values, 0).astype(bf16)
-                if p < sections - 1:
-                    patch_out[p, start : start + 16, :] = patch
-                else:
-                    patch_in[section, start : start + 16, :] = patch
-        for p, target in enumerate(targets[:-1]):
+                    terms = [share * x[i : i + 8] for share, x in zip(shares, moved)]
+                    terms.append(shares[-1] * base[i : i + 8].astype(f32))
+                    values.append(take(total(terms), turn))
+                patch_out[r * sections + p, rows, :] = jnp.concatenate(values, 0).astype(bf16)
+
+    def send_patch(r, p, a, b):
+        @pl.when((section != p) | (r != rows_axis - 1))
+        def _():
             pltpu.make_async_remote_copy(
-                src_ref=patch_out.at[p, pl.ds(a, b - a)],
+                src_ref=patch_out.at[r * sections + p, pl.ds(a, b - a)],
                 dst_ref=patch_in.at[section, pl.ds(a, b - a)],
                 send_sem=patch_send,
                 recv_sem=patch_recv.at[section],
-                device_id={"sec": target},
+                device_id={"sec": p, "row": r},
                 device_id_type=MESH,
             ).start()
 
@@ -415,28 +437,25 @@
         aligned_groups.add(g)
         return now, after
 
-    def above(c):
-        group(chunks[c][0] // 8 - 1)
-
-    def groups(c, part=None):
+    loaded = 0
+
+    def need(row):
+        nonlocal loaded
+        while not loaded or pieces[loaded - 1][0] > row:
+            loads[loaded].wait()
+            loaded += 1
+
+    def groups(c):
         a, b = chunks[c][0] // 8, chunks[c][1] // 8
-        todo = list(range(a, b))
-        if part is not None:
-            half = (b - a) // 2 - 1
-            todo = todo[:half] if part == 0 else todo[half:]
-        for g in todo:
-            if g in aligned_groups:
-                compare(g)
-            else:
-                compare(g, *group(g))
-
-    def finish_and_fill(c):
-        finish(*chunks[c])
-        fill_blocks(c)
+        for g in range(b - 1, max(a, 1) - 2, -1):
+            if g not in aligned_groups:
+                need(g * 8)
+                group(g)
+        for g in range(a, b):
+            compare(g)
 
     def halo_rows():
-        shown = jnp.where(me == 0, 0.0, 1.0)
-        rows = [shown * jnp.broadcast_to(halo_in[v], (8, LANES)) for v in range(blocks)]
+        rows = [jnp.broadcast_to(halo_in[v], (8, LANES)) for v in range(blocks)]
         turned = [take(x, to_right) for x in rows]
         for v in range(blocks):
             follows = v + 1 - per_seg if v % per_seg == per_seg - 1 else v + 1
@@ -445,70 +464,153 @@
         energies[0:8, :] = total(x * x for x in rows)
 
     last = len(chunks) - 1
-    loads[0].wait()
-    for copy in small_copies[1:]:
-        copy.wait()
-    sources.update(find_sources())
-    above(0)
     groups(0)
     for v in range(blocks):
         halo_out[v, :, :] = aligned[v + 1, row_count : row_count + 8, :]
-    finish_and_fill(0)
-    pl.semaphore_wait(barrier, owners + sections - 2)
-    send_blocks(0)
-    halo.start()
-    for load in loads[1:]:
-        load.wait()
-    weigh()
-    above(1)
-    groups(1)
-    for c in range(1, last):
-        finish_and_fill(c)
-        if c < last - 1:
-            above(c + 1)
-            groups(c + 1, 0)
+    for copy in small_copies[1:]:
+        copy.wait()
+    find_sources()
+    for p in range(sections):
+        spots_out[p : p + 1, :] = jnp.full((1, LANES), columns[0, p]).astype(f32)
+    entered = (owners - 1) + (sections - 1) * (1 + (rows_axis - 1) * (row_at // (rows_axis - 1)))
+    pl.semaphore_wait(barrier, entered)
+
+    @pl.when(me < owners - 1)
+    def _():
+        halo.start()
+
+    @pl.when(row_at != rows_axis - 1)
+    def _():
+        spots_copy.start()
+
+    early = range(last - 2)
+    rest = [(r, c) for r in range(1, rows_axis) for c in range(last + 1) if c not in early]
+    for c in range(last):
+        now = [(r, c) for r in range(rows_axis if c in early else 1)]
+        finish(*chunks[c])
+        for r, c in now:
+            fill_blocks(1, r, c)
+        if c == 0:
+            send_blocks(1, now)
+        if c + 1 < last:
+            groups(c + 1)
         else:
             group(0)
-            own_part(*chunks[0])
-        send_blocks(c)
-        if c < last - 1:
-            groups(c + 1, 1)
-    halo.wait_recv()
+        if c:
+            send_blocks(1, now)
+
+    @pl.when(me > 0)
+    def _():
+        halo.wait_recv()
+
+    @pl.when(me == 0)
+    def _():
+        halo_in[...] = jnp.zeros((blocks, 1, LANES), f32)
+
     halo_rows()
-    groups(last)
-    finish_and_fill(last)
-    send_blocks(last)
-    for c in range(1, last + 1):
-        own_part(*chunks[c])
-    for c in range(last + 1):
-        send_patches(c)
+    for g in range(chunks[last][1] // 8):
+        compare(g)
+    finish(*chunks[last])
+    fill_blocks(1, 0, last)
+    send_blocks(1, [(0, last)])
+    fill_base([0])
+
+    @pl.when(row_at != rows_axis - 1)
+    def _():
+        base_copies[0].start()
+
+    def send_all(step, sent):
+        for r, c in sent:
+            fill_blocks(step, r, c)
+        send_blocks(step, sent)
+
+    send_all(0, [(0, c) for c in range(last + 1)])
+    send_all(1, rest)
+    send_all(0, [(r, c) for r in range(1, rows_axis) for c in range(last + 1)])
+    for step in range(2, tiles):
+        send_all(step, [(r, c) for r in range(rows_axis) for c in range(last + 1)])
+    fill_base(range(1, sections))
+
+    @pl.when(row_at != rows_axis - 1)
+    def _():
+        base_copies[1].start()
+
+    @pl.when(blends)
+    def _():
+        for i in range(rows_axis - 1):
+            side_copy(spots_out, spots_in.at[i], 0).wait_recv()
+        for r in range(rows_axis):
+            weigh(r)
+        for i in range(rows_axis - 1):
+            side_copy(base_out.at[pl.ds(0, 1)], base_in.at[i, pl.ds(0, 1)], 1).wait_recv()
+        order = [(r, c) for c in early for r in range(rows_axis)]
+        order += [(0, c) for c in range(last + 1) if c not in early] + rest
+        for r, c in order:
+            wait_blocks(r, c)
+            blend(r, [0], *chunks[c])
+            send_patch(r, 0, *chunks[c])
+        for i in range(rows_axis - 1):
+            side_copy(
+                base_out.at[pl.ds(1, sections - 1)], base_in.at[i, pl.ds(1, sections - 1)], 2
+            ).wait_recv()
+        for r in range(rows_axis):
+            blend(r, list(range(1, sections)), 0, row_count)
+            for p in range(1, sections):
+                send_patch(r, p, 0, row_count)
 
     jitter_out[...] = 2.0 * jitter_rows[...].T[0:1, :]
     table_copy.wait()
-    for s in range(sections):
-
-        @pl.when(section != s)
-        def _():
-            pltpu.make_async_copy(patch_in.at[s], patch_in.at[s], patch_recv.at[s]).wait()
-
-        if s > 1:
-            early_out[s - 2] = surface(freq[s - 2], freq[s - 1], tables)
-        spectrum = forward(patch_in[s], tables)
-        freq[s] = spectrum
-        if s > sections - 3:
-            freq_out[s - sections + 2] = spectrum
-
-    halo.wait_send()
-    pltpu.make_async_copy(outbox, outbox, block_send).wait()
-    pltpu.make_async_copy(patch_out, patch_out, patch_send).wait()
-
-
-def correlate(freq, tables, jitter, early, jitter_out, surfaces_out, late, sem):
+    down = downward(section, sections)
+    done = 0
+    for batch in [[0]] + [list(range(i, min(i + 2, sections))) for i in range(1, sections, 2)]:
+        order = [i + down * (sections - 1 - 2 * i) for i in batch]
+        for s in order:
+
+            @pl.when((section != s) | (row_at != rows_axis - 1))
+            def _():
+                pltpu.make_async_copy(patch_in.at[s], patch_in.at[s], patch_recv.at[s]).wait()
+
+            @pl.when((section == s) & (row_at == rows_axis - 1))
+            def _():
+                patch_in[s] = patch_out[(rows_axis - 1) * sections + s]
+
+        spectra = [forward(patch_in[s], tables) for s in order]
+        while done < batch[0] - 1:
+            pair = done + down * (sections - 2 - 2 * done)
+            early_out[pair - down] = surface(freq[pair], freq[pair + 1], tables)
+            done += 1
+        for s, spectrum in zip(order, spectra):
+            freq[s] = spectrum
+    last_pair = (1 - down) * (sections - 2)
+    freq_out[0] = freq[last_pair]
+    freq_out[1] = freq[last_pair + 1]
+
+    @pl.when(me < owners - 1)
+    def _():
+        halo.wait_send()
+
+    @pl.when(row_at != rows_axis - 1)
+    def _():
+        pltpu.make_async_copy(outbox, outbox, block_send).wait()
+        spots_copy.wait_send()
+        for copy in base_copies:
+            copy.wait_send()
+
+    @pl.when(blends)
+    def _():
+        sent = outbox.at[pl.ds(1, tiles - 1)]
+        pltpu.make_async_copy(sent, sent, block_send).wait()
+        sent = patch_out.at[pl.ds(0, rows_axis * sections - 1)]
+        pltpu.make_async_copy(sent, sent, patch_send).wait()
+
+
+def correlate(sections, freq, tables, jitter, early, jitter_out, surfaces_out, late, sem):
     pairs = early.shape[0]
+    down = downward(lax.axis_index("sec"), sections)
     copies = [
-        pltpu.make_async_copy(early, surfaces_out.at[pl.ds(0, pairs), 0, 0], sem.at[0]),
+        pltpu.make_async_copy(early, surfaces_out.at[pl.ds(down, pairs), 0, 0], sem.at[0]),
         pltpu.make_async_copy(jitter, jitter_out, sem.at[1]),
-        pltpu.make_async_copy(late, surfaces_out.at[pairs, 0, 0], sem.at[2]),
+        pltpu.make_async_copy(late, surfaces_out.at[(1 - down) * pairs, 0, 0], sem.at[2]),
     ]
     copies[0].start()
     copies[1].start()
@@ -528,6 +630,7 @@
     chunks = len(row_chunks(row_count))
     pieces = len(load_pieces(row_count))
     sizes = (sections, tiles, rows_axis, row_count, row_width, moves)
+    spots = -(-sections // 8) * 8
     tables = dft_tables(PATCH)
     f32, bf16 = jnp.float32, jnp.bfloat16
     vmem = pl.BlockSpec(memory_space=pltpu.VMEM)
@@ -557,11 +660,14 @@
             pltpu.VMEM((row_count, LANES), f32),
             pltpu.VMEM((blocks, 8, LANES), f32),
             pltpu.VMEM((blocks, 1, LANES), f32),
-            pltpu.VMEM((owners - 1, CAP, BLOCK, BLOCK), bf16),
-            pltpu.VMEM((owners - 1, CAP, BLOCK, BLOCK), bf16),
-            pltpu.VMEM((sections, owners * CAP + 1, 8, LANES), f32),
-            pltpu.VMEM((sections, PATCH, LANES), f32),
-            pltpu.VMEM((sections - 1, PATCH, PATCH), bf16),
+            pltpu.VMEM((tiles, rows_axis, CAP, BLOCK, BLOCK), bf16),
+            pltpu.VMEM((rows_axis, owners - 1, CAP, BLOCK, BLOCK), bf16),
+            pltpu.VMEM((spots, LANES), f32),
+            pltpu.VMEM((rows_axis - 1, spots, LANES), f32),
+            pltpu.VMEM((sections, PATCH, PATCH), bf16),
+            pltpu.VMEM((rows_axis - 1, sections, PATCH, PATCH), bf16),
+            pltpu.VMEM((rows_axis, sections, owners * CAP + 1, 8, LANES), f32),
+            pltpu.VMEM((rows_axis * sections, PATCH, PATCH), bf16),
             pltpu.VMEM((sections, PATCH, PATCH), bf16),
             pltpu.VMEM((sections, 2 * PATCH, PATCH), f32),
             dma((pieces,)),
@@ -569,7 +675,9 @@
             dma((4,)),
             dma((2,)),
             dma,
-            dma((chunks,)),
+            dma((rows_axis, chunks)),
+            dma((3,)),
+            dma((3,)),
             dma,
             dma((sections,)),
         ],
@@ -587,7 +695,7 @@
         pltpu.with_memory_space_constraint(x, pltpu.VMEM) for x in between
     ]
     return pl.pallas_call(
-        correlate,
+        functools.partial(correlate, sections),
         out_shape=(
             jax.ShapeDtypeStruct((1, row_count), f32),
             jax.ShapeDtypeStruct((sections - 1, 1, 1, PATCH, PATCH), f32),

time: 16.8 us -> 16.1 us (0.958)
  the two profiles are of different devices: /device:TPU:0 before, /device:TPU:9 now
where the time goes in v3:
time: 16.1 us; the launch traced here: 16 us
  Pallas kernels  15.3 us (95%)
  between operations  0.64 us (4%)
    pallas_call x1, Pallas kernels, per_device(): pl.pallas_call(functools.partial(kernel, sizes), out_shape=(pltpu.VMEM((1...  14.2 us
    pallas_call x1, Pallas kernels, per_device(): pl.pallas_call(functools.partial(correlate, sections), out_shape=(jax.Sha...  1.1 us

profile of v3, /device:TPU:9, one launch (start us, length us, event | category | flops | bytes accessed | tf_op | source)
XLA Modules:
  0.0 16.0 jit_solution(10861508925537096665)
XLA Ops:
  0.6 14.2 %section_patches.1 = (f32[1,128]{1,0:T(1,128)S(1)}, f32[2,256,128]{2,1,0:T(8,128)S(1)}, f32[2,128,128]{2,1,0:T(8,128)S(1)}, bf16[2,384,256]{2,1,0:T(8,128)(2,1)S(1)}) custom-call(f32[1,128,4096]{2,1,0:T(8,128)} %pixels.1, s32[1,128]{1,0:T(1,128)} %delays_hbm.1, s32[1,3,4,8]{3,2,1,0:T(4,128)} %bitcast.1, f32[1,4,8]{2,1,0:T(4,128)} %weights_hbm.1, ...), custom_call_target="tpu_custom_call" | custom-call | tf_op jit(solution)/shard_map/section_patches/pallas_call | solution.py:639
  14.9 1.1 %section_correlation.1 = (f32[1,128]{1,0:T(1,128)}, f32[3,1,1,128,128]{4,3,2,1,0:T(8,128)}) custom-call(f32[2,256,128]{2,1,0:T(8,128)S(1)} %get-tuple-element.6.freq, bf16[2,384,256]{2,1,0:T(8,128)(2,1)S(1)} %get-tuple-element.7.tables, f32[1,128]{1,0:T(1,128)S(1)} %get-tuple-element.8.jitter, f32[2,128,128]{2,1,0:T(8,128)S(1)} %get-tuple-element.9.early), custom_call_target="tpu_custom_call" | custom-call | tf_op jit(solution)/shard_map/section_correlation/pallas_call | solution.py:697

commit v4 on v3

--- a/solution.py
+++ b/solution.py
@@ -67,29 +67,40 @@
 
 
 def load_pieces(row_count):
-    cuts = [row_count] + list(range(row_count - 24, 0, -32))
-    return [(a, b) for a, b in zip(cuts[1:-1] + [0], cuts[:-1])]
+    cuts = [row_count, row_count - 24, 0]
+    return list(zip(cuts[1:], cuts[:-1]))
 
 
 def downward(section, sections):
     return (section + sections - 1) // sections
 
 
-def forward(patch, tables):
+def forward(patches, tables):
     wide = tables[0, 0:PATCH, :], tables[1, 0:PATCH, :]
     square = tables[0, PATCH : 3 * PATCH, :], tables[1, PATCH : 3 * PATCH, :]
-    first = dot(patch, wide[0]) + dot(patch, wide[1])
-    stacked = jnp.concatenate([first[:, :PATCH], first[:, PATCH:]], 0)
-    return dot3(square, split(stacked))
-
-
-def surface(now, after, tables):
+    values = jnp.concatenate(patches, 0)
+    first = dot(values, wide[0]) + dot(values, wide[1])
+    stacked = [
+        jnp.concatenate([first[at : at + PATCH, :PATCH], first[at : at + PATCH, PATCH:]], 0)
+        for at in range(0, len(patches) * PATCH, PATCH)
+    ]
+    high, low = split(jnp.concatenate(stacked, 1))
+    if len(patches) > 1:
+        both = dot3(square, (high, low))
+        return [both[:, at : at + PATCH] for at in range(0, len(patches) * PATCH, PATCH)]
+    both = dot(square[0], jnp.concatenate([high, low], 1))
+    return [both[:, :PATCH] + (both[:, PATCH:] + dot(square[1], high))]
+
+
+def surface(now, after, tables, sign=None):
     wide = tables[0, 0:PATCH, :]
     square = tables[0, PATCH : 3 * PATCH, :]
     now_real, now_imag = now[0:PATCH], now[PATCH : 2 * PATCH]
     next_real, next_imag = after[0:PATCH], after[PATCH : 2 * PATCH]
     cross_real = now_real * next_real + now_imag * next_imag
     cross_imag = now_imag * next_real - now_real * next_imag
+    if sign is not None:
+        cross_imag = sign * cross_imag
     magnitude = jnp.sqrt(cross_real * cross_real + cross_imag * cross_imag)
     mean = jnp.sum(jnp.sum(magnitude, axis=0, keepdims=True), axis=1, keepdims=True) * (
         1.0 / (PATCH * PATCH)
@@ -110,8 +121,7 @@
     columns_hbm,
     tables_hbm,
     jitter_out,
-    freq_out,
-    early_out,
+    surfaces,
     tables,
     raw,
     delays,
@@ -163,6 +173,7 @@
     def band_device(band):
         return {"tile": band // rows_axis, "row": band % rows_axis}
 
+    last = len(chunks) - 1
     blends = row_at == rows_axis - 1
     others = [i + (i + owners - me) // owners for i in range(owners - 1)]
 
@@ -308,24 +319,30 @@
         jitter_rows[a:b, :] = 0.5 * jitter
 
     def fill_blocks(step, r, c):
-        a, b = chunks[c]
+        a, b = span(r, c)
         for rank in range(CAP):
             for start in range(a, b, 16):
                 block = sources[step, r, rank]
                 pair = [corrected(block, start + half) for half in (0, 8)]
                 outbox[step, r, rank, start : start + 16, :] = jnp.concatenate(pair, 0).astype(bf16)
 
+    def span(r, c):
+        return (0, chunks[c][1]) if r and c == last - 1 else chunks[c]
+
+    def landing(r, c):
+        return c + r * (last + 1) - max(r - 1, 0)
+
     def send_blocks(step, sent):
         at = tile_at(step)
 
         def start():
             for r, c in sent:
-                a, b = chunks[c]
+                a, b = span(r, c)
                 pltpu.make_async_remote_copy(
                     src_ref=outbox.at[step, r, :, pl.ds(a, b - a)],
                     dst_ref=arrived.at[r, place_at(at), :, pl.ds(a, b - a)],
                     send_sem=block_send,
-                    recv_sem=block_recv.at[r, c],
+                    recv_sem=block_recv.at[landing(r, c)],
                     device_id=blender(at),
                     device_id_type=MESH,
                 ).start()
@@ -397,9 +414,9 @@
                 coefs[r, p, i] = share * scale
 
     def wait_blocks(r, c):
-        a, b = chunks[c]
+        a, b = span(r, c)
         landed = arrived.at[r, :, :, pl.ds(a, b - a)]
-        pltpu.make_async_copy(landed, landed, block_recv.at[r, c]).wait()
+        pltpu.make_async_copy(landed, landed, block_recv.at[landing(r, c)]).wait()
 
     def blend(r, patches, a, b):
         turns = [(lane + spot(r, p)[0]) & (LANES - 1) for p in patches]
@@ -463,7 +480,6 @@
             ahead[v, 0:8, :] = jnp.where(last_lane, turned[follows], turned[v])
         energies[0:8, :] = total(x * x for x in rows)
 
-    last = len(chunks) - 1
     groups(0)
     for v in range(blocks):
         halo_out[v, :, :] = aligned[v + 1, row_count : row_count + 8, :]
@@ -483,8 +499,8 @@
     def _():
         spots_copy.start()
 
-    early = range(last - 2)
-    rest = [(r, c) for r in range(1, rows_axis) for c in range(last + 1) if c not in early]
+    early = range(last - 1)
+    rest = [(r, last - 1) for r in range(1, rows_axis)]
     for c in range(last):
         now = [(r, c) for r in range(rows_axis if c in early else 1)]
         finish(*chunks[c])
@@ -526,9 +542,10 @@
 
     send_all(0, [(0, c) for c in range(last + 1)])
     send_all(1, rest)
-    send_all(0, [(r, c) for r in range(1, rows_axis) for c in range(last + 1)])
+    later = [(r, c) for r in range(1, rows_axis) for c in range(last)]
+    send_all(0, later)
     for step in range(2, tiles):
-        send_all(step, [(r, c) for r in range(rows_axis) for c in range(last + 1)])
+        send_all(step, [(0, c) for c in range(last + 1)] + later)
     fill_base(range(1, sections))
 
     @pl.when(row_at != rows_axis - 1)
@@ -544,18 +561,36 @@
         for i in range(rows_axis - 1):
             side_copy(base_out.at[pl.ds(0, 1)], base_in.at[i, pl.ds(0, 1)], 1).wait_recv()
         order = [(r, c) for c in early for r in range(rows_axis)]
-        order += [(0, c) for c in range(last + 1) if c not in early] + rest
+        order += [(0, c) for c in range(last + 1) if c not in early]
         for r, c in order:
             wait_blocks(r, c)
-            blend(r, [0], *chunks[c])
-            send_patch(r, 0, *chunks[c])
+            blend(r, [0], *span(r, c))
+            send_patch(r, 0, *span(r, c))
         for i in range(rows_axis - 1):
             side_copy(
                 base_out.at[pl.ds(1, sections - 1)], base_in.at[i, pl.ds(1, sections - 1)], 2
             ).wait_recv()
-        for r in range(rows_axis):
-            blend(r, list(range(1, sections)), 0, row_count)
-            for p in range(1, sections):
+        others_at = list(range(1, sections))
+        blend(0, others_at, 0, row_count)
+
+        @pl.when(section == 0)
+        def _():
+            for p in others_at[::-1]:
+                send_patch(0, p, 0, row_count)
+
+        for r, c in rest:
+            wait_blocks(r, c)
+            blend(r, [0], *span(r, c))
+            send_patch(r, 0, *span(r, c))
+        for r in range(1, rows_axis):
+            blend(r, others_at, 0, row_count)
+        for p in others_at:
+
+            @pl.when(section > 0)
+            def _():
+                send_patch(0, p, 0, row_count)
+
+            for r in range(1, rows_axis):
                 send_patch(r, p, 0, row_count)
 
     jitter_out[...] = 2.0 * jitter_rows[...].T[0:1, :]
@@ -574,16 +609,18 @@
             def _():
                 patch_in[s] = patch_out[(rows_axis - 1) * sections + s]
 
-        spectra = [forward(patch_in[s], tables) for s in order]
+        spectra = forward([patch_in[s] for s in order], tables)
         while done < batch[0] - 1:
             pair = done + down * (sections - 2 - 2 * done)
-            early_out[pair - down] = surface(freq[pair], freq[pair + 1], tables)
+            surfaces[pair] = surface(freq[pair], freq[pair + 1], tables)
             done += 1
-        for s, spectrum in zip(order, spectra):
-            freq[s] = spectrum
-    last_pair = (1 - down) * (sections - 2)
-    freq_out[0] = freq[last_pair]
-    freq_out[1] = freq[last_pair + 1]
+        for i, s, spectrum in zip(batch, order, spectra):
+            if i == sections - 1:
+                pair = done + down * (sections - 2 - 2 * done)
+                sign = (1 - 2 * down).astype(f32)
+                surfaces[pair] = surface(freq[pair + down], spectrum, tables, sign)
+            else:
+                freq[s] = spectrum
 
     @pl.when(me < owners - 1)
     def _():
@@ -604,18 +641,13 @@
         pltpu.make_async_copy(sent, sent, patch_send).wait()
 
 
-def correlate(sections, freq, tables, jitter, early, jitter_out, surfaces_out, late, sem):
-    pairs = early.shape[0]
-    down = downward(lax.axis_index("sec"), sections)
+def deliver(jitter, surfaces, jitter_out, surfaces_out, sem):
     copies = [
-        pltpu.make_async_copy(early, surfaces_out.at[pl.ds(down, pairs), 0, 0], sem.at[0]),
+        pltpu.make_async_copy(surfaces, surfaces_out.at[:, 0, 0], sem.at[0]),
         pltpu.make_async_copy(jitter, jitter_out, sem.at[1]),
-        pltpu.make_async_copy(late, surfaces_out.at[(1 - down) * pairs, 0, 0], sem.at[2]),
     ]
-    copies[0].start()
-    copies[1].start()
-    late[...] = surface(freq[0], freq[1], tables)
-    copies[2].start()
+    for copy in copies:
+        copy.start()
     for copy in copies:
         copy.wait()
 
@@ -640,13 +672,12 @@
         functools.partial(kernel, sizes),
         out_shape=(
             pltpu.VMEM((1, row_count), f32),
-            pltpu.VMEM((2, 2 * PATCH, PATCH), f32),
-            pltpu.VMEM((sections - 2, PATCH, PATCH), f32),
-            pltpu.VMEM(tables.shape, bf16),
+            pltpu.VMEM((sections - 1, PATCH, PATCH), f32),
         ),
         in_specs=[anywhere] * 6,
-        out_specs=(vmem,) * 4,
+        out_specs=(vmem,) * 2,
         scratch_shapes=[
+            pltpu.VMEM(tables.shape, bf16),
             pltpu.VMEM((row_count, row_width), f32),
             pltpu.VMEM(jitter_index.shape, jnp.int32),
             pltpu.SMEM((1, 3, owners, moves), jnp.int32),
@@ -675,7 +706,7 @@
             dma((4,)),
             dma((2,)),
             dma,
-            dma((rows_axis, chunks)),
+            dma((rows_axis * chunks - (rows_axis - 1),)),
             dma((3,)),
             dma((3,)),
             dma,
@@ -691,20 +722,18 @@
         patch_col,
         tables,
     )
-    jitter, freq, early, tables = [
-        pltpu.with_memory_space_constraint(x, pltpu.VMEM) for x in between
-    ]
+    jitter, surfaces = [pltpu.with_memory_space_constraint(x, pltpu.VMEM) for x in between]
     return pl.pallas_call(
-        functools.partial(correlate, sections),
+        deliver,
         out_shape=(
             jax.ShapeDtypeStruct((1, row_count), f32),
             jax.ShapeDtypeStruct((sections - 1, 1, 1, PATCH, PATCH), f32),
         ),
-        in_specs=[vmem] * 4,
+        in_specs=[vmem] * 2,
         out_specs=(anywhere, anywhere),
-        scratch_shapes=[pltpu.VMEM((PATCH, PATCH), f32), dma((3,))],
-        name="section_correlation",
-    )(freq, tables, jitter, early)
+        scratch_shapes=[dma((2,))],
+        name="section_surfaces",
+    )(jitter, surfaces)
 
 
 def solution(mesh):

time: 16.1 us -> 15.8 us (0.981)
  the two profiles are of different devices: /device:TPU:9 before, /device:TPU:1 now
where the time goes in v4:
time: 15.8 us; the launch traced here: 15.6 us
  Pallas kernels  15 us (95%)
  between operations  0.64 us (4%)
    pallas_call x1, Pallas kernels, per_device(): pl.pallas_call(functools.partial(kernel, sizes), out_shape=(pltpu.VMEM((1...  14.3 us
    pallas_call x1, Pallas kernels, per_device(): pl.pallas_call(deliver, out_shape=(jax.ShapeDtypeStruct((1, row_count), f...  0.7 us

profile of v4, /device:TPU:1, one launch (start us, length us, event | category | flops | bytes accessed | tf_op | source)
XLA Modules:
  0.0 15.6 jit_solution(5992174612963864078)
XLA Ops:
  0.6 14.3 %section_patches.1 = (f32[1,128]{1,0:T(1,128)S(1)}, f32[3,128,128]{2,1,0:T(8,128)S(1)}) custom-call(f32[1,128,4096]{2,1,0:T(8,128)} %pixels.1, s32[1,128]{1,0:T(1,128)} %delays_hbm.1, s32[1,3,4,8]{3,2,1,0:T(4,128)} %bitcast.1, f32[1,4,8]{2,1,0:T(4,128)} %weights_hbm.1, s32[1,4]{1,0:T(1,128)} %columns_hbm.1, bf16[2,384,256]{2,1,0:T(8,128)(2,1)} %constant.2.clone.tables_hbm), custom_call_target="tpu_custom_call" | custom-call | tf_op jit(solution)/shard_map/section_patches/pallas_call | solution.py:671
  14.9 0.7 %section_surfaces.1 = (f32[1,128]{1,0:T(1,128)}, f32[3,1,1,128,128]{4,3,2,1,0:T(8,128)}) custom-call(f32[1,128]{1,0:T(1,128)S(1)} %get-tuple-element.4.jitter, f32[3,128,128]{2,1,0:T(8,128)S(1)} %get-tuple-element.5.surfaces), custom_call_target="tpu_custom_call" | custom-call | tf_op jit(solution)/shard_map/section_surfaces/pallas_call | solution.py:726

commit v5 on v4

--- a/solution.py
+++ b/solution.py
@@ -499,21 +499,21 @@
     def _():
         spots_copy.start()
 
+    def send_all(step, sent):
+        for r, c in sent:
+            fill_blocks(step, r, c)
+        send_blocks(step, sent)
+
     early = range(last - 1)
     rest = [(r, last - 1) for r in range(1, rows_axis)]
     for c in range(last):
         now = [(r, c) for r in range(rows_axis if c in early else 1)]
         finish(*chunks[c])
-        for r, c in now:
-            fill_blocks(1, r, c)
-        if c == 0:
-            send_blocks(1, now)
+        send_all(1, now)
         if c + 1 < last:
             groups(c + 1)
         else:
             group(0)
-        if c:
-            send_blocks(1, now)
 
     @pl.when(me > 0)
     def _():
@@ -534,11 +534,6 @@
     @pl.when(row_at != rows_axis - 1)
     def _():
         base_copies[0].start()
-
-    def send_all(step, sent):
-        for r, c in sent:
-            fill_blocks(step, r, c)
-        send_blocks(step, sent)
 
     send_all(0, [(0, c) for c in range(last + 1)])
     send_all(1, rest)

time: 15.8 us -> 15.3 us (0.968)
  the two profiles are of different devices: /device:TPU:1 before, /device:TPU:0 now
where the time goes in v5:
time: 15.3 us; the launch traced here: 15.1 us
  Pallas kernels  14.5 us (95%)
  between operations  0.64 us (4%)
    pallas_call x1, Pallas kernels, per_device(): pl.pallas_call(functools.partial(kernel, sizes), out_shape=(pltpu.VMEM((1...  13.8 us
    pallas_call x1, Pallas kernels, per_device(): pl.pallas_call(deliver, out_shape=(jax.ShapeDtypeStruct((1, row_count), f...  0.7 us

profile of v5, /device:TPU:0, one launch (start us, length us, event | category | flops | bytes accessed | tf_op | source)
XLA Modules:
  0.0 15.1 jit_solution(16283637239208078107)
XLA Ops:
  0.6 13.8 %section_patches.1 = (f32[1,128]{1,0:T(1,128)S(1)}, f32[3,128,128]{2,1,0:T(8,128)S(1)}) custom-call(f32[1,128,4096]{2,1,0:T(8,128)} %pixels.1, s32[1,128]{1,0:T(1,128)} %delays_hbm.1, s32[1,3,4,8]{3,2,1,0:T(4,128)} %bitcast.1, f32[1,4,8]{2,1,0:T(4,128)} %weights_hbm.1, s32[1,4]{1,0:T(1,128)} %columns_hbm.1, bf16[2,384,256]{2,1,0:T(8,128)(2,1)} %constant.2.clone.tables_hbm), custom_call_target="tpu_custom_call" | custom-call | tf_op jit(solution)/shard_map/section_patches/pallas_call | solution.py:666
  14.4 0.7 %section_surfaces.1 = (f32[1,128]{1,0:T(1,128)}, f32[3,1,1,128,128]{4,3,2,1,0:T(8,128)}) custom-call(f32[1,128]{1,0:T(1,128)S(1)} %get-tuple-element.4.jitter, f32[3,128,128]{2,1,0:T(8,128)S(1)} %get-tuple-element.5.surfaces), custom_call_target="tpu_custom_call" | custom-call | tf_op jit(solution)/shard_map/section_surfaces/pallas_call | solution.py:721

commit v6 on v5

--- a/solution.py
+++ b/solution.py
@@ -529,6 +529,7 @@
     finish(*chunks[last])
     fill_blocks(1, 0, last)
     send_blocks(1, [(0, last)])
+    send_all(1, rest)
     fill_base([0])
 
     @pl.when(row_at != rows_axis - 1)
@@ -536,7 +537,6 @@
         base_copies[0].start()
 
     send_all(0, [(0, c) for c in range(last + 1)])
-    send_all(1, rest)
     later = [(r, c) for r in range(1, rows_axis) for c in range(last)]
     send_all(0, later)
     for step in range(2, tiles):

time: 15.3 us -> 15.3 us (level)
  no operation moved by 1% of the time
where the time goes in v6:
time: 15.3 us; the launch traced here: 15.1 us
  Pallas kernels  14.5 us (95%)
  between operations  0.64 us (4%)
    pallas_call x1, Pallas kernels, per_device(): pl.pallas_call(functools.partial(kernel, sizes), out_shape=(pltpu.VMEM((1...  13.8 us
    pallas_call x1, Pallas kernels, per_device(): pl.pallas_call(deliver, out_shape=(jax.ShapeDtypeStruct((1, row_count), f...  0.7 us

profile of v6, /device:TPU:0, one launch (start us, length us, event | category | flops | bytes accessed | tf_op | source)
XLA Modules:
  0.0 15.1 jit_solution(2673705994024185304)
XLA Ops:
  0.6 13.8 %section_patches.1 = (f32[1,128]{1,0:T(1,128)S(1)}, f32[3,128,128]{2,1,0:T(8,128)S(1)}) custom-call(f32[1,128,4096]{2,1,0:T(8,128)} %pixels.1, s32[1,128]{1,0:T(1,128)} %delays_hbm.1, s32[1,3,4,8]{3,2,1,0:T(4,128)} %bitcast.1, f32[1,4,8]{2,1,0:T(4,128)} %weights_hbm.1, s32[1,4]{1,0:T(1,128)} %columns_hbm.1, bf16[2,384,256]{2,1,0:T(8,128)(2,1)} %constant.2.clone.tables_hbm), custom_call_target="tpu_custom_call" | custom-call | tf_op jit(solution)/shard_map/section_patches/pallas_call | solution.py:666
  14.4 0.7 %section_surfaces.1 = (f32[1,128]{1,0:T(1,128)}, f32[3,1,1,128,128]{4,3,2,1,0:T(8,128)}) custom-call(f32[1,128]{1,0:T(1,128)S(1)} %get-tuple-element.4.jitter, f32[3,128,128]{2,1,0:T(8,128)S(1)} %get-tuple-element.5.surfaces), custom_call_target="tpu_custom_call" | custom-call | tf_op jit(solution)/shard_map/section_surfaces/pallas_call | solution.py:721
